TPU v7x, 256 devices: a whole 4x4x8 slice. The times are simulated.
256 devices in a mesh: row: 32 (over y, z_hi, x), col: 8 (over z_lo, core).
Axes of the slice: x: 4, y: 4, z: 8 (z_hi: 2, z_lo: 4; z = z_hi * 4 + z_lo), core: 2. Of those that a mesh axis runs over, the one named last changes fastest.
Arguments:
- tokens: bfloat16 [2048, 8192], P('row', 'col'), may hold values from -6 to 6
- gate_up: bfloat16 [8192, 2, 16384], P('col', None, 'row'), may hold values from -0.0625 to 0.0625
- cotangent: bfloat16 [2048, 16384], P('col', 'row'), may hold values from -6 to 6
Outputs:
- hidden: bfloat16 [2048, 16384], P('col', 'row')
- input_grad: bfloat16 [2048, 8192], P('row', 'col')
- weight_grad: bfloat16 [8192, 2, 16384], P('col', None, 'row')
All inputs are finite; a program needn't handle non-finite values.
Results may differ from a plain program's by a relative error of at most 0.0049.
Values may be sent and summed in bfloat16 or wider, within the bound.
No kernel may reach another device: no remote copies, remote signals or barrier semaphores. Data moves between devices by JAX's collectives and lax.ppermute only.
A program may use at most 128 MiB of HBM per device.

v0:
```python
import jax
import jax.numpy as jnp
from jax import lax
from jax.sharding import PartitionSpec as P


def on_device(tokens, gate_up, cotangent):
    local_feats = tokens.shape[1]
    local_hidden = gate_up.shape[2]
    gathered = lax.all_gather(tokens, "row", axis=0, tiled=True)
    total_rows = gathered.shape[0]
    weights = gate_up.reshape(local_feats, 2 * local_hidden)
    fragment = gathered
    combined = lax.psum_scatter(
        jnp.dot(fragment, weights, preferred_element_type=jnp.float32),
        "col",
        scatter_dimension=0,
        tiled=True,
    )
    gate_pre = combined[:, :local_hidden]
    up_pre = combined[:, local_hidden:]
    sigmoid = jax.nn.sigmoid(gate_pre)
    activated = gate_pre * sigmoid
    hidden = (activated * up_pre).astype(jnp.bfloat16)
    grad_out = cotangent.astype(jnp.float32)
    grad_gate = grad_out * up_pre * sigmoid * (1.0 + gate_pre * (1.0 - sigmoid))
    grad_up = grad_out * activated
    stacked = jnp.stack([grad_gate, grad_up], axis=1).astype(jnp.bfloat16)
    all_grads = lax.all_gather(stacked, "col", axis=0, tiled=True).reshape(
        total_rows, 2 * local_hidden
    )
    weight_grad = lax.dot_general(
        gathered, all_grads, (((0,), (0,)), ((), ())), preferred_element_type=jnp.float32
    )
    weight_grad = weight_grad.astype(jnp.bfloat16).reshape(local_feats, 2, local_hidden)
    fragment = all_grads
    input_grad = lax.psum_scatter(
        lax.dot_general(
            fragment, weights, (((1,), (1,)), ((), ())), preferred_element_type=jnp.float32
        ),
        "row",
        scatter_dimension=0,
        tiled=True,
    ).astype(jnp.bfloat16)
    return (hidden, input_grad, weight_grad)


def solution(mesh):
    in_specs = (P("row", "col"), P("col", None, "row"), P("col", "row"))
    out_specs = (P("col", "row"), P("row", "col"), P("col", None, "row"))
    return jax.shard_map(
        on_device, mesh=mesh, in_specs=in_specs, out_specs=out_specs, check_vma=False
    )
```

profile of v0, /device:TPU:32, one launch (start us, length us, event | category | flops | bytes accessed | tf_op | source)
XLA Modules:
  0.0 557.2 jit_solution(3880604939707711133)
XLA Ops:
  7.2 0.0 all-gather.3.cloned.1.call-start
  7.2 0.7 all-gather.3.cloned.1.call-update
  7.9 0.0 reduce-scatter.3.cloned.1.call-start
  7.9 2.1 copy.11
  10.1 115.0 %all-gather.3.cloned.1.call-done = bf16[2048,1024]{1,0:T(8,128)(2,1)} async-done(((bf16[64,1024]{1,0:T(8,128)(2,1)}), bf16[2048,1024]{1,0:T(8,128)(2,1)}) %all-gather.3.cloned.1.call-update) | async-done | bytes 4194320 | tf_op jit(solution)/shard_map/all_gather | solution.py:10
  125.1 9.0 %fusion.8 = f32[2048,1024]{1,0:T(8,128)} fusion(bf16[2048,1024]{1,0:T(8,128)(2,1)} %all-gather.3.cloned.1.call-done, bf16[1024,1024]{1,0:T(8,128)(2,1)S(1)} %bitcast.19), kind=kOutput, calls=%fused_computation.15 | convolution fusion | flops 4294967296 | bytes 14680064 | tf_op jit(solution)/shard_map/dot_general | solution.py:15
  134.1 0.0 copy-start.1
  134.1 0.0 reduce-scatter.3.cloned.1.call-update
  134.1 0.0 all-gather.5.cloned.1.call-start
  134.2 85.8 %reduce-scatter.3.cloned.1.call-done = f32[256,1024]{1,0:T(8,128)} async-done(((f32[2048,1024]{1,0:T(8,128)}), f32[256,1024]{1,0:T(8,128)}) %reduce-scatter.3.cloned.1.call-update) | async-done | bytes 1048592 | tf_op jit(solution)/shard_map/reduce_scatter | solution.py:14
  220.0 0.0 copy-done.1
  220.0 2.2 fusion.7
  222.3 0.8 pad_maximum_fusion
  223.1 0.0 all-gather.5.cloned.1.call-update
  223.1 0.0 reduce-scatter.5.cloned.1.call-start
  223.2 53.1 %all-gather.5.cloned.1.call-done = bf16[2048,2,512]{2,0,1:T(8,128)(2,1)} async-done(((bf16[256,2,512]{2,0,1:T(8,128)(2,1)}), bf16[2048,2,512]{2,0,1:T(8,128)(2,1)}) %all-gather.5.cloned.1.call-update) | async-done | bytes 4194320 | tf_op jit(solution)/shard_map/all_gather | solution.py:29
  276.3 0.0 copy-done
  276.3 9.2 %convolution_bitcast_fusion = f32[2048,1024]{1,0:T(8,128)} fusion(bf16[2048,2,512]{2,0,1:T(8,128)(2,1)} %all-gather.5.cloned.1.call-done, bf16[1024,2,512]{2,1,0:T(2,128)(2,1)S(1)} %copy-done), kind=kOutput, calls=%fused_computation | convolution fusion | flops 4294967296 | bytes 14680064 | tf_op jit(solution)/shard_map/dot_general | solution.py:38
  285.5 0.0 reduce-scatter.5.cloned.1.call-update
  285.5 6.3 %copy.9 = bf16[2048,2,512]{0,2,1:T(8,128)(2,1)} copy(bf16[2048,2,512]{2,0,1:T(8,128)(2,1)} %all-gather.5.cloned.1.call-done) | data formatting | bytes 8388608 | tf_op jit(solution)/shard_map/all_gather | solution.py:29
  291.8 7.9 %convolution_convert_fusion = bf16[1024,1024]{1,0:T(8,128)(2,1)S(1)} fusion(bf16[2048,1024]{0,1:T(8,128)(2,1)} %bitcast.17, bf16[2048,1024]{1,0:T(8,128)(2,1)} %all-gather.3.cloned.1.call-done), kind=kOutput, calls=%fused_computation.2 | convolution fusion | flops 4296015872 | bytes 10485760 | tf_op jit(solution)/shard_map/dot_general | solution.py:32
  299.8 4.0 copy.10
  303.8 245.3 %reduce-scatter.5.cloned.1.call-done = f32[64,1024]{1,0:T(8,128)} async-done(((f32[2048,1024]{1,0:T(8,128)}), f32[64,1024]{1,0:T(8,128)}) %reduce-scatter.5.cloned.1.call-update) | async-done | bytes 262160 | tf_op jit(solution)/shard_map/reduce_scatter | solution.py:37
  549.1 1.6 convert_element_type.18
  (1 shorter events, 0.0 us)
Async XLA Ops:
  7.2 117.9 %all-gather.3.cloned.1.call-start = ((), (), s32[]{:S(2)}) async-start(), calls=%async_computation.2 | async-start | bytes 4325376 | tf_op jit(solution)/shard_map/all_gather | solution.py:10
  7.9 212.1 %reduce-scatter.3.cloned.1.call-start = ((), (), s32[]{:S(2)}) async-start(), calls=%async_computation.3 | async-start | bytes 9437184 | tf_op jit(solution)/shard_map/reduce_scatter | solution.py:14
  134.1 85.9 %copy-start.1 = (bf16[256,512]{1,0:T(8,128)(2,1)S(1)}, bf16[256,512]{1,0:T(8,128)(2,1)}, u32[]{:S(2)}) copy-start(bf16[256,512]{1,0:T(8,128)(2,1)} %param.5) | copy-start | bytes 786436
  134.1 142.2 %copy-start = (bf16[1024,2,512]{2,1,0:T(2,128)(2,1)S(1)}, bf16[1024,2,512]{2,1,0:T(2,128)(2,1)}, u32[]{:S(2)}) copy-start(bf16[1024,2,512]{2,1,0:T(2,128)(2,1)} %param.4) | copy-start | bytes 6291460
  134.1 142.1 %all-gather.5.cloned.1.call-start = ((), (), s32[]{:S(2)}) async-start(), calls=%async_computation.4 | async-start | bytes 4718592 | tf_op jit(solution)/shard_map/all_gather | solution.py:29
  223.1 325.9 %reduce-scatter.5.cloned.1.call-start = ((), (), s32[]{:S(2)}) async-start(), calls=%async_computation.5 | async-start | bytes 8650752 | tf_op jit(solution)/shard_map/reduce_scatter | solution.py:37
Sparse Core Ops, SparseCore 0:
  11.4 113.6 all-gather.2
  134.2 85.7 reduce-scatter.2
  223.3 52.9 all-gather.4
  285.7 263.3 reduce-scatter.4
where the time goes:
time: 558 us; the launch traced here: 557 us
  waiting for transfers between devices  500 us (90%)
  matrix products  26.2 us (5%)
  between operations  13.8 us (2%)
  local copies, waits for them, and re-layouts  12.5 us (2%)
    reduce_scatter x1, waiting for transfers between devices, on_device(): lax.psum_scatter(lax.dot_general(fragment, weights, (((1,), (1,)), ((), (...  245 us
    all_gather x1, waiting for transfers between devices, on_device(): gathered = lax.all_gather(tokens, 'row', axis=0, tiled=True)  115 us
    reduce_scatter x1, waiting for transfers between devices, on_device(): lax.psum_scatter(jnp.dot(fragment, weights, preferred_element_type=jnp.fl...  85.8 us
    all_gather x1, waiting for transfers between devices, on_device(): lax.all_gather(stacked, 'col', axis=0, tiled=True)  53.1 us
  transfers between devices with their start and end apart: 4, of which 4 were waited for; matrix products, arithmetic and copies ran while one was open for 4% of the time, Pallas kernels for 0%

commit v1 on v0

v1 whole, which is shorter than its diff:
```python
import jax
import jax.numpy as jnp
from jax import lax
from jax.sharding import Mesh
from jax.sharding import PartitionSpec as P

AXES = ("y", "zh", "x", "zl", "c")
CHUNKS = 1
BF16 = jnp.bfloat16
F32 = jnp.float32


def xor_perm(n, k):
    return [(i, i ^ k) for i in range(n)]


def plane_perm(k, x_core):
    pairs = []
    for y in range(4):
        for x in range(4):
            for c in range(2):
                y2, x2 = (y, x ^ k) if c == x_core else (y ^ k, x)
                pairs.append(((y * 4 + x) * 2 + c, (y2 * 4 + x2) * 2 + c))
    return pairs


def send_plane(value, k, x_core):
    return lax.ppermute(value, ("y", "x", "c"), plane_perm(k, x_core))


def pick(value, index):
    return lax.dynamic_index_in_dim(value, index, 0, keepdims=False)


def xor_rows(value, index):
    return jnp.stack([pick(value, index ^ k) for k in range(4)])


def on_device(tokens, gate_up, cotangent):
    rows, feats = tokens.shape
    half = gate_up.shape[2]
    y, zh, x, zl, c = (lax.axis_index(a) for a in AXES)
    shift = y ^ zl
    same = zh == c
    core0 = c == 0
    fwd_a, fwd_b = [(0, 2), (3, 1), (1, 0), (2, 3)], [(1, 2), (2, 1)]
    back_a = [(b, a) for a, b in fwd_a]

    recv_a = lax.ppermute(tokens, ("zh", "c"), fwd_a)
    recv_b = lax.ppermute(tokens, ("zh", "c"), fwd_b)
    own = jnp.where(same, tokens, recv_a)
    sib = jnp.where(same, recv_a, recv_b)
    block = jnp.concatenate([own, sib], axis=1)

    w_own = gate_up.reshape(feats, 2 * half)
    w_sib = lax.ppermute(w_own, "c", xor_perm(2, 1))
    weights = jnp.concatenate([w_own, w_sib], axis=0)

    line = jnp.stack([block] + [send_plane(block, k, 0) for k in (1, 2, 3)])
    size = rows // CHUNKS
    cot = xor_rows(cotangent.reshape(4, rows, half), x)

    hiddens, in_grads, toks, gs = [], [], [], []
    for j in range(CHUNKS):
        part = lax.slice_in_dim(line, j * size, (j + 1) * size, axis=1)
        plane = jnp.stack([part] + [send_plane(part, k, 1) for k in (1, 2, 3)])
        flat = plane.reshape(16 * size, 2 * feats)
        pre = jnp.dot(flat, weights, preferred_element_type=F32)
        pre = pre.reshape(4, 4, size, 2 * half)

        def slab(k):
            major = lax.dynamic_index_in_dim(pre, shift ^ k, 0, keepdims=False)
            minor = lax.dynamic_index_in_dim(pre, shift ^ k, 1, keepdims=False)
            return jnp.where(core0, major, minor)

        total = slab(0)
        for k in (1, 2, 3):
            total = total + lax.ppermute(
                slab(k).astype(BF16), "zl", xor_perm(4, k)
            ).astype(F32)
        gate_pre, up_pre = total[..., :half], total[..., half:]
        sigmoid = jax.nn.sigmoid(gate_pre)
        activated = gate_pre * sigmoid
        hiddens.append((activated * up_pre).astype(BF16))
        grad_out = lax.slice_in_dim(cot, j * size, (j + 1) * size, axis=1).astype(F32)
        grad_gate = grad_out * up_pre * sigmoid * (1.0 + gate_pre * (1.0 - sigmoid))
        grad_up = grad_out * activated
        grads = jnp.concatenate([grad_gate, grad_up], axis=-1).astype(BF16)

        gathered = jnp.stack(
            [grads] + [lax.ppermute(grads, "zl", xor_perm(4, k)) for k in (1, 2, 3)]
        )
        ordered = xor_rows(gathered, shift)
        ordered = jnp.where(core0, ordered, jnp.swapaxes(ordered, 0, 1))
        g_flat = ordered.reshape(16 * size, 2 * half)
        out = lax.dot_general(
            g_flat, weights, (((1,), (1,)), ((), ())), preferred_element_type=F32
        ).reshape(4, 4, size, 2 * feats)
        for send in (1, 0):
            part = out[0]
            for k in (1, 2, 3):
                part = part + send_plane(out[k].astype(BF16), k, send).astype(F32)
            out = part
        g_own, g_sib = out[:, :feats].astype(BF16), out[:, feats:].astype(BF16)
        recv_a = lax.ppermute(jnp.where(same, g_sib, g_own), ("zh", "c"), back_a)
        recv_b = lax.ppermute(g_sib, ("zh", "c"), fwd_b)
        first = jnp.where(same, out[:, :feats], recv_b.astype(F32))
        in_grads.append((first + recv_a.astype(F32)).astype(BF16))
        toks.append(flat)
        gs.append(g_flat)

    t_all, g_all = jnp.concatenate(toks, axis=0), jnp.concatenate(gs, axis=0)
    t_sib = lax.ppermute(t_all[:, feats:], "c", xor_perm(2, 1))
    g_sib = lax.ppermute(g_all, "c", xor_perm(2, 1))

    def outer(t, g):
        return lax.dot_general(t, g, (((0,), (0,)), ((), ())), preferred_element_type=F32)

    weight_grad = outer(t_all[:, :feats], g_all) + outer(t_sib, g_sib)
    weight_grad = weight_grad.astype(BF16).reshape(feats, 2, half)
    hidden = xor_rows(jnp.concatenate(hiddens, axis=1), x).reshape(4 * rows, half)
    return hidden, jnp.concatenate(in_grads, axis=0), weight_grad


def solution(mesh):
    split = Mesh(mesh.devices.reshape(4, 2, 4, 4, 2), AXES)
    row, col = ("y", "zh", "x"), ("zl", "c")
    in_specs = (P(row, col), P(col, None, row), P(col, row))
    out_specs = (P(col, row), P(row, col), P(col, None, row))
    return jax.shard_map(
        on_device, mesh=split, in_specs=in_specs, out_specs=out_specs, check_vma=False
    )
```

time: 558 us -> 234 us (0.42)
  the two profiles are of different devices: /device:TPU:32 before, /device:TPU:1 now
where the time goes in v1:
time: 234 us
  waiting for transfers between devices  126 us (54%)
  starting transfers between devices  69.2 us (30%)
  matrix products  16 us (7%)
  local copies, waits for them, and re-layouts  12 us (5%)
  other arithmetic  10.2 us (4%)
    ppermute x12, waiting for transfers between devices, send_plane(): return lax.ppermute(value, ('y', 'x', 'c'), plane_perm(k, x_core))  52.7 us
    ppermute x3, waiting for transfers between devices, on_device(): lax.ppermute(slab(k).astype(BF16), 'zl', xor_perm(4, k)).astype(F32)  34.7 us
    ppermute x3, waiting for transfers between devices, on_device(): lax.ppermute(grads, 'zl', xor_perm(4, k))  33 us
    ppermute x3, starting transfers between devices, on_device(): lax.ppermute(grads, 'zl', xor_perm(4, k))  23.8 us
    ppermute x12, starting transfers between devices, send_plane(): return lax.ppermute(value, ('y', 'x', 'c'), plane_perm(k, x_core))  15.7 us
    ppermute x1, starting transfers between devices, on_device(): recv_b = lax.ppermute(g_sib, ('zh', 'c'), fwd_b)  12.4 us
    unnamed x13, local copies, waits for them, and re-layouts  9.19 us
    ppermute x1, starting transfers between devices, on_device(): recv_b = lax.ppermute(tokens, ('zh', 'c'), fwd_b)  7.36 us
  transfers between devices with their start and end apart: 25, of which 17 were waited for; matrix products, arithmetic and copies ran while one was open for 3% of the time, Pallas kernels for 0%

profile of v1, /device:TPU:1, one launch (start us, length us, event | category | flops | bytes accessed | tf_op | source)
XLA Modules:
  0.0 234.1 jit_solution(15902258597121444703)
XLA Ops:
  2.8 3.3 %collective-permute-start.8 = (bf16[1024,1024]{1,0:T(8,128)(2,1)S(1)}, bf16[1024,1024]{1,0:T(8,128)(2,1)}, u32[]{:S(2)}, u32[]{:S(2)}) collective-permute-start(bf16[1024,1024]{1,0:T(8,128)(2,1)S(1)} %bitcast.82), channel_id=1, source_target_pairs={{0,1},{1,0},{2,3},{3,2},{4,5},{5,4},{6,7},{7,6},{8,9},{9,8},{10,11... | collective-permute-start | bytes 6291464 | tf_op jit(solution)/shard_map/ppermute | solution.py:56
  6.3 7.4 %collective-permute-start.1 = (bf16[64,1024]{1,0:T(8,128)(2,1)S(1)}, bf16[64,1024]{1,0:T(8,128)(2,1)S(1)}, u32[]{:S(2)}, u32[]{:S(2)}) collective-permute-start(bf16[64,1024]{1,0:T(8,128)(2,1)S(1)} %copy-done.4), channel_id=1, source_target_pairs={{1,32},{32,1},{3,34},{34,3},{5,36},{36,5},{7,38},{38,7},{9,40},{40... | collective-permute-start | bytes 393224 | tf_op jit(solution)/shard_map/ppermute | solution.py:50
  14.0 3.1 %collective-permute-done.1 = bf16[64,1024]{1,0:T(8,128)(2,1)S(1)} collective-permute-done((bf16[64,1024]{1,0:T(8,128)(2,1)S(1)}, bf16[64,1024]{1,0:T(8,128)(2,1)S(1)}, u32[]{:S(2)}, u32[]{:S(2)}) %collective-permute-start.1) | collective-permute-done | bytes 131104 | tf_op jit(solution)/shard_map/ppermute | solution.py:50
  17.2 3.2 %collective-permute-start.3 = (bf16[64,2048]{1,0:T(8,128)(2,1)S(1)}, bf16[64,2048]{1,0:T(8,128)(2,1)S(1)}, u32[]{:S(2)}, u32[]{:S(2)}) collective-permute-start(bf16[64,2048]{1,0:T(8,128)(2,1)S(1)} %get-tuple-element.37), channel_id=1, source_target_pairs={{0,16},{1,129},{8,24},{9,137},{16,0},{17,145},{24,8},{25,153},{64,... | collective-permute-start | bytes 786440 | tf_op jit(solution)/shard_map/ppermute | solution.py:28
  21.2 3.0 %collective-permute-done.3 = bf16[64,2048]{1,0:T(8,128)(2,1)S(1)} collective-permute-done((bf16[64,2048]{1,0:T(8,128)(2,1)S(1)}, bf16[64,2048]{1,0:T(8,128)(2,1)S(1)}, u32[]{:S(2)}, u32[]{:S(2)}) %collective-permute-start.3) | collective-permute-done | bytes 262176 | tf_op jit(solution)/shard_map/ppermute | solution.py:28
  24.1 3.2 %collective-permute-done.2 = bf16[64,2048]{1,0:T(8,128)(2,1)S(1)} collective-permute-done((bf16[64,2048]{1,0:T(8,128)(2,1)S(1)}, bf16[64,2048]{1,0:T(8,128)(2,1)S(1)}, u32[]{:S(2)}, u32[]{:S(2)}) %collective-permute-start.2) | collective-permute-done | bytes 262176 | tf_op jit(solution)/shard_map/ppermute | solution.py:28
  28.5 2.7 %collective-permute-start.6 = (bf16[4,64,2048]{2,1,0:T(8,128)(2,1)}, bf16[4,64,2048]{2,1,0:T(8,128)(2,1)}, u32[]{:S(2)}, u32[]{:S(2)}) collective-permute-start(bf16[4,64,2048]{2,1,0:T(8,128)(2,1)} %get-tuple-element.27), channel_id=1, source_target_pairs={{0,128},{1,17},{8,136},{9,25},{16,144},{17,1},{24,152},{25,9},{64,... | collective-permute-start | bytes 3145736 | tf_op jit(solution)/shard_map/ppermute | solution.py:28
  34.1 10.2 %collective-permute-done.6 = bf16[4,64,2048]{2,1,0:T(8,128)(2,1)} collective-permute-done((bf16[4,64,2048]{2,1,0:T(8,128)(2,1)}, bf16[4,64,2048]{2,1,0:T(8,128)(2,1)}, u32[]{:S(2)}, u32[]{:S(2)}) %collective-permute-start.6) | collective-permute-done | bytes 1048608 | tf_op jit(solution)/shard_map/ppermute | solution.py:28
  44.3 11.3 %collective-permute-done.5 = bf16[4,64,2048]{2,1,0:T(8,128)(2,1)} collective-permute-done((bf16[4,64,2048]{2,1,0:T(8,128)(2,1)}, bf16[4,64,2048]{2,1,0:T(8,128)(2,1)}, u32[]{:S(2)}, u32[]{:S(2)}) %collective-permute-start.5) | collective-permute-done | bytes 1048608 | tf_op jit(solution)/shard_map/ppermute | solution.py:28
  55.7 6.3 %fusion = f32[4,4,64,1024]{3,2,1,0:T(8,128)S(1)} fusion(bf16[2048,1024]{1,0:T(8,128)(2,1)S(1)} %constant_dynamic-update-slice_fusion, bf16[1,4,64,2048]{3,2,1,0:T(8,128)(2,1)} %bitcast.7, bf16[1,4,64,2048]{3,2,1,0:T(8,128)(2,1)} %bitcast.6, bf16[1,4,64,2048]{3,2,1,0:T(8,128)(2,1)} %bitcast.5, bf16[1,4,64,2048]{3,2,1,0:T(8,128)(2,1)S(1)} %get-tuple-element.26), kind=kOutput, calls=%fused_computation.1 | convolution fusion | flops 4301258752 | bytes 12582912 | tf_op jit(solution)/shard_map/dot_general | solution.py:68
  67.9 19.6 %collective-permute-done.9 = bf16[4,64,1024]{2,1,0:T(8,128)(2,1)S(1)} collective-permute-done((bf16[4,64,1024]{2,1,0:T(8,128)(2,1)}, bf16[4,64,1024]{2,1,0:T(8,128)(2,1)S(1)}, u32[]{:S(2)}, u32[]{:S(2)}) %collective-permute-start.9) | collective-permute-done | bytes 524320 | tf_op jit(solution)/shard_map/ppermute | solution.py:78
  88.4 14.2 %collective-permute-done.11 = bf16[4,64,1024]{2,1,0:T(8,128)(2,1)} collective-permute-done((bf16[4,64,1024]{2,1,0:T(8,128)(2,1)S(1)}, bf16[4,64,1024]{2,1,0:T(8,128)(2,1)}, u32[]{:S(2)}, u32[]{:S(2)}) %collective-permute-start.11) | collective-permute-done | bytes 524320 | tf_op jit(solution)/shard_map/ppermute | solution.py:78
  107.0 21.8 %collective-permute-start.13 = (bf16[4,64,1024]{2,1,0:T(8,128)(2,1)S(1)}, bf16[4,64,1024]{2,1,0:T(8,128)(2,1)S(1)}, u32[]{:S(2)}, u32[]{:S(2)}) collective-permute-start(bf16[4,64,1024]{2,1,0:T(8,128)(2,1)S(1)} %pad_maximum_fusion.4), channel_id=1, source_target_pairs={{0,4},{2,6},{4,0},{6,2},{1,5},{3,7},{5,1},{7,3},{8,12},{10,14},{12... | collective-permute-start | bytes 1572872 | tf_op jit(solution)/shard_map/ppermute | solution.py:91
  129.0 32.9 %collective-permute-done.13 = bf16[4,64,1024]{2,1,0:T(8,128)(2,1)S(1)} collective-permute-done((bf16[4,64,1024]{2,1,0:T(8,128)(2,1)S(1)}, bf16[4,64,1024]{2,1,0:T(8,128)(2,1)S(1)}, u32[]{:S(2)}, u32[]{:S(2)}) %collective-permute-start.13) | collective-permute-done | bytes 524320 | tf_op jit(solution)/shard_map/ppermute | solution.py:91
  164.8 4.6 %fusion.25 = (bf16[1024,2048]{1,0:T(8,128)(2,1)S(1)}, f32[1024,2048]{1,0:T(8,128)S(1)}) fusion(bf16[1024,1024]{1,0:T(8,128)(2,1)S(1)} %bitcast.88, bf16[2048,1024]{1,0:T(8,128)(2,1)S(1)} %copy-done.2), kind=kOutput, calls=%fused_computation.65 | convolution fusion | flops 4297064448 | bytes 18874368 | tf_op jit(solution)/shard_map/dot_general | solution.py:96
  169.6 3.2 %collective-permute-start.17 = (bf16[4,64,2048]{2,1,0:T(8,128)(2,1)S(1)}, bf16[4,64,2048]{2,1,0:T(8,128)(2,1)S(1)}, u32[]{:S(2)}, u32[]{:S(2)}) collective-permute-start(bf16[4,64,2048]{2,1,0:T(8,128)(2,1)S(1)} %bitcast.94), channel_id=1, source_target_pairs={{0,192},{1,25},{8,200},{9,17},{16,208},{17,9},{24,216},{25,1},{64,... | collective-permute-start | bytes 3145736 | tf_op jit(solution)/shard_map/ppermute | solution.py:28
  176.5 2.6 %collective-permute-start.23 = (bf16[1024,1024]{1,0:T(8,128)(2,1)S(1)}, bf16[1024,1024]{1,0:T(8,128)(2,1)S(1)}, u32[]{:S(2)}, u32[]{:S(2)}) collective-permute-start(bf16[1024,1024]{1,0:T(8,128)(2,1)S(1)} %slice.81), channel_id=1, source_target_pairs={{0,1},{1,0},{2,3},{3,2},{4,5},{5,4},{6,7},{7,6},{8,9},{9,8},{10,11... | collective-permute-start | bytes 6291464 | tf_op jit(solution)/shard_map/ppermute | solution.py:113
  179.5 5.9 %collective-permute-done.17 = bf16[4,64,2048]{2,1,0:T(8,128)(2,1)S(1)} collective-permute-done((bf16[4,64,2048]{2,1,0:T(8,128)(2,1)S(1)}, bf16[4,64,2048]{2,1,0:T(8,128)(2,1)S(1)}, u32[]{:S(2)}, u32[]{:S(2)}) %collective-permute-start.17) | collective-permute-done | bytes 1048608 | tf_op jit(solution)/shard_map/ppermute | solution.py:28
  186.8 11.1 %collective-permute-done.16 = bf16[4,64,2048]{2,1,0:T(8,128)(2,1)S(1)} collective-permute-done((bf16[4,64,2048]{2,1,0:T(8,128)(2,1)S(1)}, bf16[4,64,2048]{2,1,0:T(8,128)(2,1)S(1)}, u32[]{:S(2)}, u32[]{:S(2)}) %collective-permute-start.16) | collective-permute-done | bytes 1048608 | tf_op jit(solution)/shard_map/ppermute | solution.py:28
  204.0 3.6 %collective-permute-done.20 = bf16[64,2048]{1,0:T(8,128)(2,1)S(1)} collective-permute-done((bf16[64,2048]{1,0:T(8,128)(2,1)S(1)}, bf16[64,2048]{1,0:T(8,128)(2,1)S(1)}, u32[]{:S(2)}, u32[]{:S(2)}) %collective-permute-start.20) | collective-permute-done | bytes 262176 | tf_op jit(solution)/shard_map/ppermute | solution.py:28
  209.1 12.4 %collective-permute-start.21 = (bf16[64,1024]{1,0:T(8,128)(2,1)S(1)}, bf16[64,1024]{1,0:T(8,128)(2,1)S(1)}, u32[]{:S(2)}, u32[]{:S(2)}) collective-permute-start(bf16[64,1024]{1,0:T(8,128)(2,1)S(1)} %get-tuple-element.7), channel_id=1, source_target_pairs={{1,32},{32,1},{3,34},{34,3},{5,36},{36,5},{7,38},{38,7},{9,40},{40... | collective-permute-start | bytes 393224 | tf_op jit(solution)/shard_map/ppermute | solution.py:106
  224.9 2.5 %fusion.26 = f32[1024,1024]{0,1:T(8,128)S(1)} fusion(bf16[1024,1024]{1,0:T(8,128)(2,1)S(1)} %collective-permute-done.23, bf16[1024,1024]{1,0:T(8,128)(2,1)S(1)} %collective-permute-done.24), kind=kOutput, calls=%fused_computation.66 | convolution fusion | flops 2147483648 | bytes 8388608 | tf_op jit(solution)/shard_map/dot_general | solution.py:117
  227.4 2.6 %add_convert_fusion = bf16[1024,1024]{0,1:T(8,128)(2,1)S(1)} fusion(f32[1024,1024]{0,1:T(8,128)S(1)} %fusion.26, bf16[1024,1024]{1,0:T(8,128)(2,1)S(1)} %bitcast.90, bf16[1024,2048]{1,0:T(8,128)(2,1)S(1)} %bitcast.81), kind=kOutput, calls=%fused_computation.3 | convolution fusion | flops 2149580800 | bytes 10485760 | tf_op jit(solution)/shard_map/dot_general | solution.py:117
  230.0 4.0 %copy.7 = bf16[1024,2,512]{2,1,0:T(2,128)(2,1)} copy(bf16[1024,2,512]{0,2,1:T(8,128)(2,1)S(1)} %bitcast.91) | data formatting | bytes 4194304
  (67 shorter events, 38.2 us)
Async XLA Ops:
  2.8 29.5 %collective-permute-start.8 = (bf16[1024,1024]{1,0:T(8,128)(2,1)S(1)}, bf16[1024,1024]{1,0:T(8,128)(2,1)}, u32[]{:S(2)}, u32[]{:S(2)}) collective-permute-start(bf16[1024,1024]{1,0:T(8,128)(2,1)S(1)} %bitcast.82), channel_id=1, source_target_pairs={{0,1},{1,0},{2,3},{3,2},{4,5},{5,4},{6,7},{7,6},{8,9},{9,8},{10,11... | collective-permute-start | bytes 6291464 | tf_op jit(solution)/shard_map/ppermute | solution.py:56
  6.2 7.8 %collective-permute-start = (bf16[64,1024]{1,0:T(8,128)(2,1)S(1)}, bf16[64,1024]{1,0:T(8,128)(2,1)S(1)}, u32[]{:S(2)}, u32[]{:S(2)}) collective-permute-start(bf16[64,1024]{1,0:T(8,128)(2,1)S(1)} %copy-done.4), channel_id=1, source_target_pairs={{0,32},{33,1},{1,0},{32,33},{2,34},{35,3},{3,2},{34,35},{4,36},{37... | collective-permute-start | bytes 393224 | tf_op jit(solution)/shard_map/ppermute | solution.py:49
  6.3 10.8 %collective-permute-start.1 = (bf16[64,1024]{1,0:T(8,128)(2,1)S(1)}, bf16[64,1024]{1,0:T(8,128)(2,1)S(1)}, u32[]{:S(2)}, u32[]{:S(2)}) collective-permute-start(bf16[64,1024]{1,0:T(8,128)(2,1)S(1)} %copy-done.4), channel_id=1, source_target_pairs={{1,32},{32,1},{3,34},{34,3},{5,36},{36,5},{7,38},{38,7},{9,40},{40... | collective-permute-start | bytes 393224 | tf_op jit(solution)/shard_map/ppermute | solution.py:50
  17.2 7.0 %collective-permute-start.3 = (bf16[64,2048]{1,0:T(8,128)(2,1)S(1)}, bf16[64,2048]{1,0:T(8,128)(2,1)S(1)}, u32[]{:S(2)}, u32[]{:S(2)}) collective-permute-start(bf16[64,2048]{1,0:T(8,128)(2,1)S(1)} %get-tuple-element.37), channel_id=1, source_target_pairs={{0,16},{1,129},{8,24},{9,137},{16,0},{17,145},{24,8},{25,153},{64,... | collective-permute-start | bytes 786440 | tf_op jit(solution)/shard_map/ppermute | solution.py:28
  20.4 7.0 %collective-permute-start.2 = (bf16[64,2048]{1,0:T(8,128)(2,1)S(1)}, bf16[64,2048]{1,0:T(8,128)(2,1)S(1)}, u32[]{:S(2)}, u32[]{:S(2)}) collective-permute-start(bf16[64,2048]{1,0:T(8,128)(2,1)S(1)} %get-tuple-element.37), channel_id=1, source_target_pairs={{0,8},{1,65},{8,0},{9,73},{16,24},{17,81},{24,16},{25,89},{64,72},... | collective-permute-start | bytes 786440 | tf_op jit(solution)/shard_map/ppermute | solution.py:28
  20.8 6.6 %collective-permute-start.4 = (bf16[64,2048]{1,0:T(8,128)(2,1)S(1)}, bf16[64,2048]{1,0:T(8,128)(2,1)S(1)}, u32[]{:S(2)}, u32[]{:S(2)}) collective-permute-start(bf16[64,2048]{1,0:T(8,128)(2,1)S(1)} %get-tuple-element.37), channel_id=1, source_target_pairs={{0,24},{1,193},{8,16},{9,201},{16,8},{17,209},{24,0},{25,217},{64,... | collective-permute-start | bytes 786440 | tf_op jit(solution)/shard_map/ppermute | solution.py:28
  28.5 15.8 %collective-permute-start.6 = (bf16[4,64,2048]{2,1,0:T(8,128)(2,1)}, bf16[4,64,2048]{2,1,0:T(8,128)(2,1)}, u32[]{:S(2)}, u32[]{:S(2)}) collective-permute-start(bf16[4,64,2048]{2,1,0:T(8,128)(2,1)} %get-tuple-element.27), channel_id=1, source_target_pairs={{0,128},{1,17},{8,136},{9,25},{16,144},{17,1},{24,152},{25,9},{64,... | collective-permute-start | bytes 3145736 | tf_op jit(solution)/shard_map/ppermute | solution.py:28
  31.3 24.4 %collective-permute-start.5 = (bf16[4,64,2048]{2,1,0:T(8,128)(2,1)}, bf16[4,64,2048]{2,1,0:T(8,128)(2,1)}, u32[]{:S(2)}, u32[]{:S(2)}) collective-permute-start(bf16[4,64,2048]{2,1,0:T(8,128)(2,1)} %get-tuple-element.27), channel_id=1, source_target_pairs={{0,64},{1,9},{8,72},{9,1},{16,80},{17,25},{24,88},{25,17},{64,0},{... | collective-permute-start | bytes 3145736 | tf_op jit(solution)/shard_map/ppermute | solution.py:28
  31.6 24.1 %collective-permute-start.7 = (bf16[4,64,2048]{2,1,0:T(8,128)(2,1)}, bf16[4,64,2048]{2,1,0:T(8,128)(2,1)}, u32[]{:S(2)}, u32[]{:S(2)}) collective-permute-start(bf16[4,64,2048]{2,1,0:T(8,128)(2,1)} %get-tuple-element.27), channel_id=1, source_target_pairs={{0,192},{1,25},{8,200},{9,17},{16,208},{17,9},{24,216},{25,1},{64,... | collective-permute-start | bytes 3145736 | tf_op jit(solution)/shard_map/ppermute | solution.py:28
  64.2 23.3 %collective-permute-start.9 = (bf16[4,64,1024]{2,1,0:T(8,128)(2,1)}, bf16[4,64,1024]{2,1,0:T(8,128)(2,1)S(1)}, u32[]{:S(2)}, u32[]{:S(2)}) collective-permute-start(bf16[4,64,1024]{2,1,0:T(8,128)(2,1)} %get-tuple-element.13), channel_id=1, source_target_pairs={{0,2},{2,0},{4,6},{6,4},{1,3},{3,1},{5,7},{7,5},{8,10},{10,8},{12,... | collective-permute-start | bytes 1572872 | tf_op jit(solution)/shard_map/ppermute | solution.py:78
  65.8 22.6 %collective-permute-start.10 = (bf16[4,64,1024]{2,1,0:T(8,128)(2,1)S(1)}, bf16[4,64,1024]{2,1,0:T(8,128)(2,1)S(1)}, u32[]{:S(2)}, u32[]{:S(2)}) collective-permute-start(bf16[4,64,1024]{2,1,0:T(8,128)(2,1)S(1)} %get-tuple-element.14), channel_id=1, source_target_pairs={{0,4},{2,6},{4,0},{6,2},{1,5},{3,7},{5,1},{7,3},{8,12},{10,14},{12... | collective-permute-start | bytes 1572872 | tf_op jit(solution)/shard_map/ppermute | solution.py:78
  67.0 35.6 %collective-permute-start.11 = (bf16[4,64,1024]{2,1,0:T(8,128)(2,1)S(1)}, bf16[4,64,1024]{2,1,0:T(8,128)(2,1)}, u32[]{:S(2)}, u32[]{:S(2)}) collective-permute-start(bf16[4,64,1024]{2,1,0:T(8,128)(2,1)S(1)} %get-tuple-element.15), channel_id=1, source_target_pairs={{0,6},{2,4},{4,2},{6,0},{1,7},{3,5},{5,3},{7,1},{8,14},{10,12},{12... | collective-permute-start | bytes 1572872 | tf_op jit(solution)/shard_map/ppermute | solution.py:78
  105.1 23.8 %collective-permute-start.14 = (bf16[4,64,1024]{2,1,0:T(8,128)(2,1)S(1)}, bf16[4,64,1024]{2,1,0:T(8,128)(2,1)S(1)}, u32[]{:S(2)}, u32[]{:S(2)}) collective-permute-start(bf16[4,64,1024]{2,1,0:T(8,128)(2,1)S(1)} %pad_maximum_fusion.4), channel_id=1, source_target_pairs={{0,6},{2,4},{4,2},{6,0},{1,7},{3,5},{5,3},{7,1},{8,14},{10,12},{12... | collective-permute-start | bytes 1572872 | tf_op jit(solution)/shard_map/ppermute | solution.py:91
  107.0 54.9 %collective-permute-start.13 = (bf16[4,64,1024]{2,1,0:T(8,128)(2,1)S(1)}, bf16[4,64,1024]{2,1,0:T(8,128)(2,1)S(1)}, u32[]{:S(2)}, u32[]{:S(2)}) collective-permute-start(bf16[4,64,1024]{2,1,0:T(8,128)(2,1)S(1)} %pad_maximum_fusion.4), channel_id=1, source_target_pairs={{0,4},{2,6},{4,0},{6,2},{1,5},{3,7},{5,1},{7,3},{8,12},{10,14},{12... | collective-permute-start | bytes 1572872 | tf_op jit(solution)/shard_map/ppermute | solution.py:91
  128.8 33.1 %collective-permute-start.12 = (bf16[4,64,1024]{2,1,0:T(8,128)(2,1)S(1)}, bf16[4,64,1024]{2,1,0:T(8,128)(2,1)S(1)}, u32[]{:S(2)}, u32[]{:S(2)}) collective-permute-start(bf16[4,64,1024]{2,1,0:T(8,128)(2,1)S(1)} %pad_maximum_fusion.4), channel_id=1, source_target_pairs={{0,2},{2,0},{4,6},{6,4},{1,3},{3,1},{5,7},{7,5},{8,10},{10,8},{12,... | collective-permute-start | bytes 1572872 | tf_op jit(solution)/shard_map/ppermute | solution.py:91
  169.6 15.7 %collective-permute-start.17 = (bf16[4,64,2048]{2,1,0:T(8,128)(2,1)S(1)}, bf16[4,64,2048]{2,1,0:T(8,128)(2,1)S(1)}, u32[]{:S(2)}, u32[]{:S(2)}) collective-permute-start(bf16[4,64,2048]{2,1,0:T(8,128)(2,1)S(1)} %bitcast.94), channel_id=1, source_target_pairs={{0,192},{1,25},{8,200},{9,17},{16,208},{17,9},{24,216},{25,1},{64,... | collective-permute-start | bytes 3145736 | tf_op jit(solution)/shard_map/ppermute | solution.py:28
  172.9 13.9 %collective-permute-start.15 = (bf16[4,64,2048]{2,1,0:T(8,128)(2,1)S(1)}, bf16[4,64,2048]{2,1,0:T(8,128)(2,1)S(1)}, u32[]{:S(2)}, u32[]{:S(2)}) collective-permute-start(bf16[4,64,2048]{2,1,0:T(8,128)(2,1)S(1)} %bitcast.93), channel_id=1, source_target_pairs={{0,64},{1,9},{8,72},{9,1},{16,80},{17,25},{24,88},{25,17},{64,0},{... | collective-permute-start | bytes 3145736 | tf_op jit(solution)/shard_map/ppermute | solution.py:28
  172.9 25.0 %collective-permute-start.16 = (bf16[4,64,2048]{2,1,0:T(8,128)(2,1)S(1)}, bf16[4,64,2048]{2,1,0:T(8,128)(2,1)S(1)}, u32[]{:S(2)}, u32[]{:S(2)}) collective-permute-start(bf16[4,64,2048]{2,1,0:T(8,128)(2,1)S(1)} %bitcast.92), channel_id=1, source_target_pairs={{0,128},{1,17},{8,136},{9,25},{16,144},{17,1},{24,152},{25,9},{64,... | collective-permute-start | bytes 3145736 | tf_op jit(solution)/shard_map/ppermute | solution.py:28
  176.5 48.4 %collective-permute-start.23 = (bf16[1024,1024]{1,0:T(8,128)(2,1)S(1)}, bf16[1024,1024]{1,0:T(8,128)(2,1)S(1)}, u32[]{:S(2)}, u32[]{:S(2)}) collective-permute-start(bf16[1024,1024]{1,0:T(8,128)(2,1)S(1)} %slice.81), channel_id=1, source_target_pairs={{0,1},{1,0},{2,3},{3,2},{4,5},{5,4},{6,7},{7,6},{8,9},{9,8},{10,11... | collective-permute-start | bytes 6291464 | tf_op jit(solution)/shard_map/ppermute | solution.py:113
  179.2 45.7 %collective-permute-start.24 = (bf16[1024,1024]{1,0:T(8,128)(2,1)S(1)}, bf16[1024,1024]{1,0:T(8,128)(2,1)S(1)}, u32[]{:S(2)}, u32[]{:S(2)}) collective-permute-start(bf16[1024,1024]{1,0:T(8,128)(2,1)S(1)} %bitcast.89), channel_id=1, source_target_pairs={{0,1},{1,0},{2,3},{3,2},{4,5},{5,4},{6,7},{7,6},{8,9},{9,8},{10,11... | collective-permute-start | bytes 6291464 | tf_op jit(solution)/shard_map/ppermute | solution.py:114
  199.5 8.0 %collective-permute-start.20 = (bf16[64,2048]{1,0:T(8,128)(2,1)S(1)}, bf16[64,2048]{1,0:T(8,128)(2,1)S(1)}, u32[]{:S(2)}, u32[]{:S(2)}) collective-permute-start(bf16[64,2048]{1,0:T(8,128)(2,1)S(1)} %get-tuple-element.23), channel_id=1, source_target_pairs={{0,24},{1,193},{8,16},{9,201},{16,8},{17,209},{24,0},{25,217},{64,... | collective-permute-start | bytes 786440 | tf_op jit(solution)/shard_map/ppermute | solution.py:28
  201.4 7.4 %collective-permute-start.19 = (bf16[64,2048]{1,0:T(8,128)(2,1)S(1)}, bf16[64,2048]{1,0:T(8,128)(2,1)S(1)}, u32[]{:S(2)}, u32[]{:S(2)}) collective-permute-start(bf16[64,2048]{1,0:T(8,128)(2,1)S(1)} %get-tuple-element.24), channel_id=1, source_target_pairs={{0,16},{1,129},{8,24},{9,137},{16,0},{17,145},{24,8},{25,153},{64,... | collective-permute-start | bytes 786440 | tf_op jit(solution)/shard_map/ppermute | solution.py:28
  209.0 13.3 %collective-permute-start.22 = (bf16[64,1024]{1,0:T(8,128)(2,1)S(1)}, bf16[64,1024]{1,0:T(8,128)(2,1)S(1)}, u32[]{:S(2)}, u32[]{:S(2)}) collective-permute-start(bf16[64,1024]{1,0:T(8,128)(2,1)S(1)} %get-tuple-element.6), channel_id=1, source_target_pairs={{32,0},{1,33},{0,1},{33,32},{34,2},{3,35},{2,3},{35,34},{36,4},{5,... | collective-permute-start | bytes 393224 | tf_op jit(solution)/shard_map/ppermute | solution.py:105
  209.1 15.1 %collective-permute-start.21 = (bf16[64,1024]{1,0:T(8,128)(2,1)S(1)}, bf16[64,1024]{1,0:T(8,128)(2,1)S(1)}, u32[]{:S(2)}, u32[]{:S(2)}) collective-permute-start(bf16[64,1024]{1,0:T(8,128)(2,1)S(1)} %get-tuple-element.7), channel_id=1, source_target_pairs={{1,32},{32,1},{3,34},{34,3},{5,36},{36,5},{7,38},{38,7},{9,40},{40... | collective-permute-start | bytes 393224 | tf_op jit(solution)/shard_map/ppermute | solution.py:106
  (6 other events, 49.0 us)

commit v2 on v1

--- a/solution.py
+++ b/solution.py
@@ -63,14 +63,24 @@
     hiddens, in_grads, toks, gs = [], [], [], []
     for j in range(CHUNKS):
         part = lax.slice_in_dim(line, j * size, (j + 1) * size, axis=1)
-        plane = jnp.stack([part] + [send_plane(part, k, 1) for k in (1, 2, 3)])
-        flat = plane.reshape(16 * size, 2 * feats)
-        pre = jnp.dot(flat, weights, preferred_element_type=F32)
+        near, far = send_plane(part, 1, 1), send_plane(part, 3, 1)
+        relay = [send_plane(near[:2], 3, 1), send_plane(far[2:], 1, 1)]
+
+        def rows_of(blocks):
+            return jnp.concatenate(blocks).reshape(-1, 2 * feats)
+
+        first, last = rows_of([part, near, far]), rows_of(relay)
+        flat = jnp.concatenate([first, last])
+        pre = jnp.concatenate(
+            [jnp.dot(v, weights, preferred_element_type=F32) for v in (first, last)]
+        )
         pre = pre.reshape(4, 4, size, 2 * half)
 
         def slab(k):
-            major = lax.dynamic_index_in_dim(pre, shift ^ k, 0, keepdims=False)
-            minor = lax.dynamic_index_in_dim(pre, shift ^ k, 1, keepdims=False)
+            place = shift ^ k
+            major = lax.dynamic_index_in_dim(pre, place ^ (place >> 1), 0, keepdims=False)
+            minor = lax.dynamic_index_in_dim(pre, place, 1, keepdims=False)
+            minor = jnp.concatenate([minor[:2], minor[3:], minor[2:3]])
             return jnp.where(core0, major, minor)
 
         total = slab(0)
@@ -92,15 +102,37 @@
         )
         ordered = xor_rows(gathered, shift)
         ordered = jnp.where(core0, ordered, jnp.swapaxes(ordered, 0, 1))
+        ordered = jnp.concatenate([ordered[:2], ordered[3:], ordered[2:3]])
         g_flat = ordered.reshape(16 * size, 2 * half)
-        out = lax.dot_general(
-            g_flat, weights, (((1,), (1,)), ((), ())), preferred_element_type=F32
-        ).reshape(4, 4, size, 2 * feats)
-        for send in (1, 0):
-            part = out[0]
-            for k in (1, 2, 3):
-                part = part + send_plane(out[k].astype(BF16), k, send).astype(F32)
-            out = part
+        def back(v):
+            out = lax.dot_general(
+                v, weights, (((1,), (1,)), ((), ())), preferred_element_type=F32
+            )
+            return out.reshape(-1, 4, size, 2 * feats)
+
+        cut = 12 * size
+        (relay,) = back(g_flat[cut:])
+        relay = relay.astype(BF16)
+        low, high = send_plane(relay[:2], 1, 1), send_plane(relay[2:], 3, 1)
+        out, near, far = back(g_flat[:cut])
+        far = jnp.concatenate([far[:2] + low.astype(F32), far[2:]]).astype(BF16)
+        near = jnp.concatenate([near[:2], near[2:] + high.astype(F32)]).astype(BF16)
+        recv = [send_plane(near, 1, 1), send_plane(far, 3, 1)]
+        t_sib = lax.ppermute(flat[:, feats:], "c", xor_perm(2, 1))
+        g_sib = lax.ppermute(g_flat, "c", xor_perm(2, 1))
+        weight_grad = lax.dot_general(
+            jnp.concatenate([flat[:, :feats], t_sib]),
+            jnp.concatenate([g_flat, g_sib]),
+            (((0,), (0,)), ((), ())),
+            preferred_element_type=F32,
+        )
+        weight_grad = weight_grad.astype(BF16).reshape(feats, 2, half)
+        *recv, weight_grad = lax.optimization_barrier((*recv, weight_grad))
+        out = out + recv[0].astype(F32) + recv[1].astype(F32)
+        part = out[0]
+        for k in (1, 2, 3):
+            part = part + send_plane(out[k].astype(BF16), k, 0).astype(F32)
+        out = part
         g_own, g_sib = out[:, :feats].astype(BF16), out[:, feats:].astype(BF16)
         recv_a = lax.ppermute(jnp.where(same, g_sib, g_own), ("zh", "c"), back_a)
         recv_b = lax.ppermute(g_sib, ("zh", "c"), fwd_b)
@@ -109,15 +141,6 @@
         toks.append(flat)
         gs.append(g_flat)
 
-    t_all, g_all = jnp.concatenate(toks, axis=0), jnp.concatenate(gs, axis=0)
-    t_sib = lax.ppermute(t_all[:, feats:], "c", xor_perm(2, 1))
-    g_sib = lax.ppermute(g_all, "c", xor_perm(2, 1))
-
-    def outer(t, g):
-        return lax.dot_general(t, g, (((0,), (0,)), ((), ())), preferred_element_type=F32)
-
-    weight_grad = outer(t_all[:, :feats], g_all) + outer(t_sib, g_sib)
-    weight_grad = weight_grad.astype(BF16).reshape(feats, 2, half)
     hidden = xor_rows(jnp.concatenate(hiddens, axis=1), x).reshape(4 * rows, half)
     return hidden, jnp.concatenate(in_grads, axis=0), weight_grad
 

time: 234 us -> 217 us (0.927)
  starting transfers between devices: 69.2 us -> 56 us
  waiting for transfers between devices: 126 us -> 121 us
  local copies, waits for them, and re-layouts: 12 us -> 15.7 us
    ppermute x3, starting transfers between devices: 23.8 us -> 4.01 us  [on_device(): lax.ppermute(grads, 'zl', xor_perm(4, k))]
    ppermute x12 -> x14, waiting for transfers between devices: 52.7 us -> 41.6 us  [send_plane(): return lax.ppermute(value, ('y', 'x', 'c'), plane_perm(k, x_core))]
    ppermute x2, starting transfers between devices: 2.73 us -> 11.2 us  [the longest x1 5.68 us: on_device(): t_sib = lax.ppermute(flat[:, feats:], 'c', xor_perm(2, 1))]
    ppermute x3, waiting for transfers between devices: 34.7 us -> 39.4 us  [on_device(): lax.ppermute(slab(k).astype(BF16), 'zl', xor_perm(4, k)).astype(F32)]
    another operation x4, other arithmetic: 4.38 us -> 1.13 us  [the longest x2 3.25 us: on_device(): plane = jnp.stack([part] + [send_plane(part, k, 1) for k in (1, 2, 3)])]
    ppermute x1, starting transfers between devices: 0.11 us -> 3.33 us  [on_device(): recv_a = lax.ppermute(tokens, ('zh', 'c'), fwd_a)]
    ppermute x3, waiting for transfers between devices: 33 us -> 35.9 us  [on_device(): lax.ppermute(grads, 'zl', xor_perm(4, k))]
    dot_general x4 -> x5, matrix products: 16 us -> 14 us  [the longest x2 4.73 us: back(): lax.dot_general(v, weights, (((1,), (1,)), ((), ())), preferred_element_t...]
  transfers between devices with their start and end apart: 25 -> 27, of which waited for: 17 -> 16; matrix products, arithmetic and copies ran while one was open for 3% -> 10% of each run, Pallas kernels for 0% -> 0%
where the time goes in v2:
time: 217 us
  waiting for transfers between devices  121 us (56%)
  starting transfers between devices  56 us (26%)
  local copies, waits for them, and re-layouts  15.7 us (7%)
  matrix products  14 us (6%)
  other arithmetic  8.67 us (4%)
    ppermute x14, waiting for transfers between devices, send_plane(): return lax.ppermute(value, ('y', 'x', 'c'), plane_perm(k, x_core))  41.6 us
    ppermute x3, waiting for transfers between devices, on_device(): lax.ppermute(slab(k).astype(BF16), 'zl', xor_perm(4, k)).astype(F32)  39.4 us
    ppermute x3, waiting for transfers between devices, on_device(): lax.ppermute(grads, 'zl', xor_perm(4, k))  35.9 us
    ppermute x14, starting transfers between devices, send_plane(): return lax.ppermute(value, ('y', 'x', 'c'), plane_perm(k, x_core))  13.7 us
    ppermute x1, starting transfers between devices, on_device(): recv_b = lax.ppermute(g_sib, ('zh', 'c'), fwd_b)  12.6 us
    unnamed x19, local copies, waits for them, and re-layouts  10.5 us
    ppermute x1, starting transfers between devices, on_device(): recv_b = lax.ppermute(tokens, ('zh', 'c'), fwd_b)  6.98 us
    ppermute x1, starting transfers between devices, on_device(): t_sib = lax.ppermute(flat[:, feats:], 'c', xor_perm(2, 1))  5.68 us
  transfers between devices with their start and end apart: 27, of which 16 were waited for; matrix products, arithmetic and copies ran while one was open for 10% of the time, Pallas kernels for 0%

profile of v2, /device:TPU:1, one launch (start us, length us, event | category | flops | bytes accessed | tf_op | source)
XLA Modules:
  0.0 216.7 jit_solution(4778709424263923704)
XLA Ops:
  0.6 3.3 %collective-permute-start = (bf16[64,1024]{1,0:T(8,128)(2,1)}, bf16[64,1024]{1,0:T(8,128)(2,1)S(1)}, u32[]{:S(2)}, u32[]{:S(2)}) collective-permute-start(bf16[64,1024]{1,0:T(8,128)(2,1)} %param.3), channel_id=1, source_target_pairs={{0,32},{33,1},{1,0},{32,33},{2,34},{35,3},{3,2},{34,35},{4,36},{37... | collective-permute-start | bytes 393224 | tf_op jit(solution)/shard_map/ppermute | solution.py:49
  4.0 7.0 %collective-permute-start.1 = (bf16[64,1024]{1,0:T(8,128)(2,1)}, bf16[64,1024]{1,0:T(8,128)(2,1)S(1)}, u32[]{:S(2)}, u32[]{:S(2)}) collective-permute-start(bf16[64,1024]{1,0:T(8,128)(2,1)} %param.3), channel_id=1, source_target_pairs={{1,32},{32,1},{3,34},{34,3},{5,36},{36,5},{7,38},{38,7},{9,40},{40... | collective-permute-start | bytes 393224 | tf_op jit(solution)/shard_map/ppermute | solution.py:50
  11.1 4.2 %collective-permute-done.1 = bf16[64,1024]{1,0:T(8,128)(2,1)S(1)} collective-permute-done((bf16[64,1024]{1,0:T(8,128)(2,1)}, bf16[64,1024]{1,0:T(8,128)(2,1)S(1)}, u32[]{:S(2)}, u32[]{:S(2)}) %collective-permute-start.1) | collective-permute-done | bytes 131104 | tf_op jit(solution)/shard_map/ppermute | solution.py:50
  16.1 2.9 %collective-permute-start.3 = (bf16[64,2048]{1,0:T(8,128)(2,1)}, bf16[64,2048]{1,0:T(8,128)(2,1)S(1)}, u32[]{:S(2)}, u32[]{:S(2)}) collective-permute-start(bf16[64,2048]{1,0:T(8,128)(2,1)} %get-tuple-element.59), channel_id=1, source_target_pairs={{0,16},{1,129},{8,24},{9,137},{16,0},{17,145},{24,8},{25,153},{64,... | collective-permute-start | bytes 786440 | tf_op jit(solution)/shard_map/ppermute | solution.py:28
  23.4 3.1 %collective-permute-done.2 = bf16[64,2048]{1,0:T(8,128)(2,1)S(1)} collective-permute-done((bf16[64,2048]{1,0:T(8,128)(2,1)}, bf16[64,2048]{1,0:T(8,128)(2,1)S(1)}, u32[]{:S(2)}, u32[]{:S(2)}) %collective-permute-start.2) | collective-permute-done | bytes 262176 | tf_op jit(solution)/shard_map/ppermute | solution.py:28
  26.6 2.6 %collective-permute-start.6 = (bf16[4,64,2048]{2,1,0:T(8,128)(2,1)S(1)}, bf16[4,64,2048]{2,1,0:T(8,128)(2,1)S(1)}, u32[]{:S(2)}, u32[]{:S(2)}) collective-permute-start(bf16[4,64,2048]{2,1,0:T(8,128)(2,1)S(1)} %pad_maximum_fusion.6), channel_id=1, source_target_pairs={{0,192},{1,25},{8,200},{9,17},{16,208},{17,9},{24,216},{25,1},{64,... | collective-permute-start | bytes 3145736 | tf_op jit(solution)/shard_map/ppermute | solution.py:28
  29.3 12.6 %collective-permute-done.6 = bf16[4,64,2048]{2,1,0:T(8,128)(2,1)S(1)} collective-permute-done((bf16[4,64,2048]{2,1,0:T(8,128)(2,1)S(1)}, bf16[4,64,2048]{2,1,0:T(8,128)(2,1)S(1)}, u32[]{:S(2)}, u32[]{:S(2)}) %collective-permute-start.6) | collective-permute-done | bytes 1048608 | tf_op jit(solution)/shard_map/ppermute | solution.py:28
  44.9 5.5 %collective-permute-done.9 = bf16[2,64,2048]{2,1,0:T(8,128)(2,1)S(1)} collective-permute-done((bf16[2,64,2048]{2,1,0:T(8,128)(2,1)S(1)}, bf16[2,64,2048]{2,1,0:T(8,128)(2,1)S(1)}, u32[]{:S(2)}, u32[]{:S(2)}) %collective-permute-start.9) | collective-permute-done | bytes 524320 | tf_op jit(solution)/shard_map/ppermute | solution.py:28
  50.4 2.5 %collective-permute-done.8 = bf16[2,64,2048]{2,1,0:T(8,128)(2,1)S(1)} collective-permute-done((bf16[2,64,2048]{2,1,0:T(8,128)(2,1)S(1)}, bf16[2,64,2048]{2,1,0:T(8,128)(2,1)S(1)}, u32[]{:S(2)}, u32[]{:S(2)}) %collective-permute-start.8) | collective-permute-done | bytes 524320 | tf_op jit(solution)/shard_map/ppermute | solution.py:28
  56.7 3.4 %fusion.43 = f32[768,1024]{1,0:T(8,128)S(1)} fusion(bf16[768,2048]{1,0:T(8,128)(2,1)S(1)} %bitcast.110, bf16[2048,1024]{1,0:T(8,128)(2,1)S(1)} %constant_dynamic-update-slice_fusion.6), kind=kOutput, calls=%fused_computation.107 | convolution fusion | flops 3221225472 | bytes 10485760 | tf_op jit(solution)/shard_map/dot_general | solution.py:75
  67.5 5.1 %collective-permute-done.10 = bf16[4,64,1024]{2,1,0:T(8,128)(2,1)S(1)} collective-permute-done((bf16[4,64,1024]{2,1,0:T(8,128)(2,1)S(1)}, bf16[4,64,1024]{2,1,0:T(8,128)(2,1)S(1)}, u32[]{:S(2)}, u32[]{:S(2)}) %collective-permute-start.10) | collective-permute-done | bytes 524320 | tf_op jit(solution)/shard_map/ppermute | solution.py:88
  72.7 14.5 %collective-permute-done.12 = bf16[4,64,1024]{2,1,0:T(8,128)(2,1)} collective-permute-done((bf16[4,64,1024]{2,1,0:T(8,128)(2,1)S(1)}, bf16[4,64,1024]{2,1,0:T(8,128)(2,1)}, u32[]{:S(2)}, u32[]{:S(2)}) %collective-permute-start.12) | collective-permute-done | bytes 524320 | tf_op jit(solution)/shard_map/ppermute | solution.py:88
  87.2 19.7 %collective-permute-done.11 = bf16[4,64,1024]{2,1,0:T(8,128)(2,1)} collective-permute-done((bf16[4,64,1024]{2,1,0:T(8,128)(2,1)S(1)}, bf16[4,64,1024]{2,1,0:T(8,128)(2,1)}, u32[]{:S(2)}, u32[]{:S(2)}) %collective-permute-start.11) | collective-permute-done | bytes 524320 | tf_op jit(solution)/shard_map/ppermute | solution.py:88
  109.4 3.6 %collective-permute-start.15 = (bf16[4,64,1024]{2,1,0:T(8,128)(2,1)S(1)}, bf16[4,64,1024]{2,1,0:T(8,128)(2,1)S(1)}, u32[]{:S(2)}, u32[]{:S(2)}) collective-permute-start(bf16[4,64,1024]{2,1,0:T(8,128)(2,1)S(1)} %pad_maximum_fusion.10), channel_id=1, source_target_pairs={{0,6},{2,4},{4,2},{6,0},{1,7},{3,5},{5,3},{7,1},{8,14},{10,12},{12... | collective-permute-start | bytes 1572872 | tf_op jit(solution)/shard_map/ppermute | solution.py:101
  114.0 5.7 %collective-permute-start.20 = (bf16[1024,1024]{1,0:T(8,128)(2,1)S(1)}, bf16[1024,1024]{1,0:T(8,128)(2,1)S(1)}, u32[]{:S(2)}, u32[]{:S(2)}) collective-permute-start(bf16[1024,1024]{1,0:T(8,128)(2,1)S(1)} %get-tuple-element.19), channel_id=1, source_target_pairs={{0,1},{1,0},{2,3},{3,2},{4,5},{5,4},{6,7},{7,6},{8,9},{9,8},{10,11... | collective-permute-start | bytes 6291464 | tf_op jit(solution)/shard_map/ppermute | solution.py:121
  120.7 34.9 %collective-permute-done.14 = bf16[4,64,1024]{2,1,0:T(8,128)(2,1)S(1)} collective-permute-done((bf16[4,64,1024]{2,1,0:T(8,128)(2,1)S(1)}, bf16[4,64,1024]{2,1,0:T(8,128)(2,1)S(1)}, u32[]{:S(2)}, u32[]{:S(2)}) %collective-permute-start.14) | collective-permute-done | bytes 524320 | tf_op jit(solution)/shard_map/ppermute | solution.py:101
  161.4 5.6 %collective-permute-start.21 = (bf16[1024,1024]{1,0:T(8,128)(2,1)S(1)}, bf16[1024,1024]{1,0:T(8,128)(2,1)S(1)}, u32[]{:S(2)}, u32[]{:S(2)}) collective-permute-start(bf16[1024,1024]{1,0:T(8,128)(2,1)S(1)} %bitcast.116), channel_id=1, source_target_pairs={{0,1},{1,0},{2,3},{3,2},{4,5},{5,4},{6,7},{7,6},{8,9},{9,8},{10,11... | collective-permute-start | bytes 6291464 | tf_op jit(solution)/shard_map/ppermute | solution.py:122
  166.9 3.5 %fusion.42 = (bf16[768,2048]{1,0:T(8,128)(2,1)S(1)}, f32[768,2048]{1,0:T(8,128)S(1)}) fusion(bf16[768,1024]{1,0:T(8,128)(2,1)S(1)} %bitcast.120, bf16[2048,1024]{1,0:T(8,128)(2,1)S(1)} %copy-done.4), kind=kOutput, calls=%fused_computation.106 | convolution fusion | flops 3222798336 | bytes 15204352 | tf_op jit(solution)/shard_map/dot_general | solution.py:108
  172.9 4.6 %fusion.13 = bf16[1024,1024]{0,1:T(8,128)(2,1)S(1)} fusion(bf16[1024,1024]{1,0:T(8,128)(2,1)S(1)} %collective-permute-done.21, bf16[1024,1024]{1,0:T(8,128)(2,1)S(1)} %bitcast.117, bf16[1024,1024]{1,0:T(8,128)(2,1)S(1)} %collective-permute-done.20, bf16[1024,1024]{1,0:T(8,128)(2,1)S(1)} %get-tuple-element.18), kind=kOutput, calls=%fused_computation.20 | convolution fusion | flops 4312793088 | bytes 10485760 | tf_op jit(solution)/shard_map/dot_general | solution.py:123
  177.5 7.6 %collective-permute-done.17 = bf16[4,64,2048]{2,1,0:T(8,128)(2,1)S(1)} collective-permute-done((bf16[4,64,2048]{2,1,0:T(8,128)(2,1)S(1)}, bf16[4,64,2048]{2,1,0:T(8,128)(2,1)S(1)}, u32[]{:S(2)}, u32[]{:S(2)}) %collective-permute-start.17) | collective-permute-done | bytes 1048608 | tf_op jit(solution)/shard_map/ppermute | solution.py:28
  190.6 2.3 %collective-permute-done.22 = bf16[64,2048]{1,0:T(8,128)(2,1)S(1)} collective-permute-done((bf16[64,2048]{1,0:T(8,128)(2,1)S(1)}, bf16[64,2048]{1,0:T(8,128)(2,1)S(1)}, u32[]{:S(2)}, u32[]{:S(2)}) %collective-permute-start.22) | collective-permute-done | bytes 262176 | tf_op jit(solution)/shard_map/ppermute | solution.py:28
  192.9 5.3 %collective-permute-done.24 = bf16[64,2048]{1,0:T(8,128)(2,1)S(1)} collective-permute-done((bf16[64,2048]{1,0:T(8,128)(2,1)S(1)}, bf16[64,2048]{1,0:T(8,128)(2,1)S(1)}, u32[]{:S(2)}, u32[]{:S(2)}) %collective-permute-start.24) | collective-permute-done | bytes 262176 | tf_op jit(solution)/shard_map/ppermute | solution.py:28
  198.6 12.6 %collective-permute-start.25 = (bf16[64,1024]{1,0:T(8,128)(2,1)S(1)}, bf16[64,1024]{1,0:T(8,128)(2,1)S(1)}, u32[]{:S(2)}, u32[]{:S(2)}) collective-permute-start(bf16[64,1024]{1,0:T(8,128)(2,1)S(1)} %get-tuple-element.13), channel_id=1, source_target_pairs={{1,32},{32,1},{3,34},{34,3},{5,36},{36,5},{7,38},{38,7},{9,40},{40... | collective-permute-start | bytes 393224 | tf_op jit(solution)/shard_map/ppermute | solution.py:138
  211.9 4.0 %copy.10 = bf16[1024,2,512]{2,1,0:T(2,128)(2,1)} copy(bf16[1024,2,512]{0,2,1:T(8,128)(2,1)S(1)} %bitcast.115) | data formatting | bytes 4194304
  (98 shorter events, 39.5 us)
Async XLA Ops:
  0.6 10.5 %collective-permute-start = (bf16[64,1024]{1,0:T(8,128)(2,1)}, bf16[64,1024]{1,0:T(8,128)(2,1)S(1)}, u32[]{:S(2)}, u32[]{:S(2)}) collective-permute-start(bf16[64,1024]{1,0:T(8,128)(2,1)} %param.3), channel_id=1, source_target_pairs={{0,32},{33,1},{1,0},{32,33},{2,34},{35,3},{3,2},{34,35},{4,36},{37... | collective-permute-start | bytes 393224 | tf_op jit(solution)/shard_map/ppermute | solution.py:49
  4.0 11.3 %collective-permute-start.1 = (bf16[64,1024]{1,0:T(8,128)(2,1)}, bf16[64,1024]{1,0:T(8,128)(2,1)S(1)}, u32[]{:S(2)}, u32[]{:S(2)}) collective-permute-start(bf16[64,1024]{1,0:T(8,128)(2,1)} %param.3), channel_id=1, source_target_pairs={{1,32},{32,1},{3,34},{34,3},{5,36},{36,5},{7,38},{38,7},{9,40},{40... | collective-permute-start | bytes 393224 | tf_op jit(solution)/shard_map/ppermute | solution.py:50
  19.0 7.5 %collective-permute-start.2 = (bf16[64,2048]{1,0:T(8,128)(2,1)}, bf16[64,2048]{1,0:T(8,128)(2,1)S(1)}, u32[]{:S(2)}, u32[]{:S(2)}) collective-permute-start(bf16[64,2048]{1,0:T(8,128)(2,1)} %get-tuple-element.59), channel_id=1, source_target_pairs={{0,8},{1,65},{8,0},{9,73},{16,24},{17,81},{24,16},{25,89},{64,72},... | collective-permute-start | bytes 786440 | tf_op jit(solution)/shard_map/ppermute | solution.py:28
  21.9 31.0 %collective-permute-start.7 = (bf16[1024,1024]{1,0:T(8,128)(2,1)S(1)}, bf16[1024,1024]{1,0:T(8,128)(2,1)}, u32[]{:S(2)}, u32[]{:S(2)}) collective-permute-start(bf16[1024,1024]{1,0:T(8,128)(2,1)S(1)} %bitcast.104), channel_id=1, source_target_pairs={{0,1},{1,0},{2,3},{3,2},{4,5},{5,4},{6,7},{7,6},{8,9},{9,8},{10,11... | collective-permute-start | bytes 6291464 | tf_op jit(solution)/shard_map/ppermute | solution.py:56
  26.6 15.2 %collective-permute-start.6 = (bf16[4,64,2048]{2,1,0:T(8,128)(2,1)S(1)}, bf16[4,64,2048]{2,1,0:T(8,128)(2,1)S(1)}, u32[]{:S(2)}, u32[]{:S(2)}) collective-permute-start(bf16[4,64,2048]{2,1,0:T(8,128)(2,1)S(1)} %pad_maximum_fusion.6), channel_id=1, source_target_pairs={{0,192},{1,25},{8,200},{9,17},{16,208},{17,9},{24,216},{25,1},{64,... | collective-permute-start | bytes 3145736 | tf_op jit(solution)/shard_map/ppermute | solution.py:28
  29.2 13.9 %collective-permute-start.5 = (bf16[4,64,2048]{2,1,0:T(8,128)(2,1)S(1)}, bf16[4,64,2048]{2,1,0:T(8,128)(2,1)S(1)}, u32[]{:S(2)}, u32[]{:S(2)}) collective-permute-start(bf16[4,64,2048]{2,1,0:T(8,128)(2,1)S(1)} %pad_maximum_fusion.6), channel_id=1, source_target_pairs={{0,64},{1,9},{8,72},{9,1},{16,80},{17,25},{24,88},{25,17},{64,0},{... | collective-permute-start | bytes 3145736 | tf_op jit(solution)/shard_map/ppermute | solution.py:28
  41.9 8.4 %collective-permute-start.9 = (bf16[2,64,2048]{2,1,0:T(8,128)(2,1)S(1)}, bf16[2,64,2048]{2,1,0:T(8,128)(2,1)S(1)}, u32[]{:S(2)}, u32[]{:S(2)}) collective-permute-start(bf16[2,64,2048]{2,1,0:T(8,128)(2,1)S(1)} %slice.219), channel_id=1, source_target_pairs={{0,64},{1,9},{8,72},{9,1},{16,80},{17,25},{24,88},{25,17},{64,0},{... | collective-permute-start | bytes 1572872 | tf_op jit(solution)/shard_map/ppermute | solution.py:28
  43.2 9.6 %collective-permute-start.8 = (bf16[2,64,2048]{2,1,0:T(8,128)(2,1)S(1)}, bf16[2,64,2048]{2,1,0:T(8,128)(2,1)S(1)}, u32[]{:S(2)}, u32[]{:S(2)}) collective-permute-start(bf16[2,64,2048]{2,1,0:T(8,128)(2,1)S(1)} %slice.218), channel_id=1, source_target_pairs={{0,192},{1,25},{8,200},{9,17},{16,208},{17,9},{24,216},{25,1},{64,... | collective-permute-start | bytes 1572872 | tf_op jit(solution)/shard_map/ppermute | solution.py:28
  62.7 10.0 %collective-permute-start.10 = (bf16[4,64,1024]{2,1,0:T(8,128)(2,1)S(1)}, bf16[4,64,1024]{2,1,0:T(8,128)(2,1)S(1)}, u32[]{:S(2)}, u32[]{:S(2)}) collective-permute-start(bf16[4,64,1024]{2,1,0:T(8,128)(2,1)S(1)} %get-tuple-element.20), channel_id=1, source_target_pairs={{0,2},{2,0},{4,6},{6,4},{1,3},{3,1},{5,7},{7,5},{8,10},{10,8},{12,... | collective-permute-start | bytes 1572872 | tf_op jit(solution)/shard_map/ppermute | solution.py:88
  63.9 23.3 %collective-permute-start.12 = (bf16[4,64,1024]{2,1,0:T(8,128)(2,1)S(1)}, bf16[4,64,1024]{2,1,0:T(8,128)(2,1)}, u32[]{:S(2)}, u32[]{:S(2)}) collective-permute-start(bf16[4,64,1024]{2,1,0:T(8,128)(2,1)S(1)} %get-tuple-element.21), channel_id=1, source_target_pairs={{0,6},{2,4},{4,2},{6,0},{1,7},{3,5},{5,3},{7,1},{8,14},{10,12},{12... | collective-permute-start | bytes 1572872 | tf_op jit(solution)/shard_map/ppermute | solution.py:88
  65.2 41.8 %collective-permute-start.11 = (bf16[4,64,1024]{2,1,0:T(8,128)(2,1)S(1)}, bf16[4,64,1024]{2,1,0:T(8,128)(2,1)}, u32[]{:S(2)}, u32[]{:S(2)}) collective-permute-start(bf16[4,64,1024]{2,1,0:T(8,128)(2,1)S(1)} %get-tuple-element.22), channel_id=1, source_target_pairs={{0,4},{2,6},{4,0},{6,2},{1,5},{3,7},{5,1},{7,3},{8,12},{10,14},{12... | collective-permute-start | bytes 1572872 | tf_op jit(solution)/shard_map/ppermute | solution.py:88
  109.4 11.3 %collective-permute-start.15 = (bf16[4,64,1024]{2,1,0:T(8,128)(2,1)S(1)}, bf16[4,64,1024]{2,1,0:T(8,128)(2,1)S(1)}, u32[]{:S(2)}, u32[]{:S(2)}) collective-permute-start(bf16[4,64,1024]{2,1,0:T(8,128)(2,1)S(1)} %pad_maximum_fusion.10), channel_id=1, source_target_pairs={{0,6},{2,4},{4,2},{6,0},{1,7},{3,5},{5,3},{7,1},{8,14},{10,12},{12... | collective-permute-start | bytes 1572872 | tf_op jit(solution)/shard_map/ppermute | solution.py:101
  113.1 42.5 %collective-permute-start.14 = (bf16[4,64,1024]{2,1,0:T(8,128)(2,1)S(1)}, bf16[4,64,1024]{2,1,0:T(8,128)(2,1)S(1)}, u32[]{:S(2)}, u32[]{:S(2)}) collective-permute-start(bf16[4,64,1024]{2,1,0:T(8,128)(2,1)S(1)} %pad_maximum_fusion.10), channel_id=1, source_target_pairs={{0,4},{2,6},{4,0},{6,2},{1,5},{3,7},{5,1},{7,3},{8,12},{10,14},{12... | collective-permute-start | bytes 1572872 | tf_op jit(solution)/shard_map/ppermute | solution.py:101
  113.1 42.5 %collective-permute-start.13 = (bf16[4,64,1024]{2,1,0:T(8,128)(2,1)S(1)}, bf16[4,64,1024]{2,1,0:T(8,128)(2,1)S(1)}, u32[]{:S(2)}, u32[]{:S(2)}) collective-permute-start(bf16[4,64,1024]{2,1,0:T(8,128)(2,1)S(1)} %pad_maximum_fusion.10), channel_id=1, source_target_pairs={{0,2},{2,0},{4,6},{6,4},{1,3},{3,1},{5,7},{7,5},{8,10},{10,8},{12,... | collective-permute-start | bytes 1572872 | tf_op jit(solution)/shard_map/ppermute | solution.py:101
  114.0 58.9 %collective-permute-start.20 = (bf16[1024,1024]{1,0:T(8,128)(2,1)S(1)}, bf16[1024,1024]{1,0:T(8,128)(2,1)S(1)}, u32[]{:S(2)}, u32[]{:S(2)}) collective-permute-start(bf16[1024,1024]{1,0:T(8,128)(2,1)S(1)} %get-tuple-element.19), channel_id=1, source_target_pairs={{0,1},{1,0},{2,3},{3,2},{4,5},{5,4},{6,7},{7,6},{8,9},{9,8},{10,11... | collective-permute-start | bytes 6291464 | tf_op jit(solution)/shard_map/ppermute | solution.py:121
  160.0 11.1 %collective-permute-start.18 = (bf16[2,64,2048]{2,1,0:T(8,128)(2,1)S(1)}, bf16[2,64,2048]{2,1,0:T(8,128)(2,1)S(1)}, u32[]{:S(2)}, u32[]{:S(2)}) collective-permute-start(bf16[2,64,2048]{2,1,0:T(8,128)(2,1)S(1)} %get-tuple-element.47), channel_id=1, source_target_pairs={{0,64},{1,9},{8,72},{9,1},{16,80},{17,25},{24,88},{25,17},{64,0},{... | collective-permute-start | bytes 1572872 | tf_op jit(solution)/shard_map/ppermute | solution.py:28
  160.1 10.5 %collective-permute-start.16 = (bf16[2,64,2048]{2,1,0:T(8,128)(2,1)S(1)}, bf16[2,64,2048]{2,1,0:T(8,128)(2,1)S(1)}, u32[]{:S(2)}, u32[]{:S(2)}) collective-permute-start(bf16[2,64,2048]{2,1,0:T(8,128)(2,1)S(1)} %get-tuple-element.48), channel_id=1, source_target_pairs={{0,192},{1,25},{8,200},{9,17},{16,208},{17,9},{24,216},{25,1},{64,... | collective-permute-start | bytes 1572872 | tf_op jit(solution)/shard_map/ppermute | solution.py:28
  161.4 11.6 %collective-permute-start.21 = (bf16[1024,1024]{1,0:T(8,128)(2,1)S(1)}, bf16[1024,1024]{1,0:T(8,128)(2,1)S(1)}, u32[]{:S(2)}, u32[]{:S(2)}) collective-permute-start(bf16[1024,1024]{1,0:T(8,128)(2,1)S(1)} %bitcast.116), channel_id=1, source_target_pairs={{0,1},{1,0},{2,3},{3,2},{4,5},{5,4},{6,7},{7,6},{8,9},{9,8},{10,11... | collective-permute-start | bytes 6291464 | tf_op jit(solution)/shard_map/ppermute | solution.py:122
  170.9 14.3 %collective-permute-start.17 = (bf16[4,64,2048]{2,1,0:T(8,128)(2,1)S(1)}, bf16[4,64,2048]{2,1,0:T(8,128)(2,1)S(1)}, u32[]{:S(2)}, u32[]{:S(2)}) collective-permute-start(bf16[4,64,2048]{2,1,0:T(8,128)(2,1)S(1)} %pad_maximum_fusion.8), channel_id=1, source_target_pairs={{0,64},{1,9},{8,72},{9,1},{16,80},{17,25},{24,88},{25,17},{64,0},{... | collective-permute-start | bytes 3145736 | tf_op jit(solution)/shard_map/ppermute | solution.py:28
  171.4 15.2 %collective-permute-start.19 = (bf16[4,64,2048]{2,1,0:T(8,128)(2,1)S(1)}, bf16[4,64,2048]{2,1,0:T(8,128)(2,1)S(1)}, u32[]{:S(2)}, u32[]{:S(2)}) collective-permute-start(bf16[4,64,2048]{2,1,0:T(8,128)(2,1)S(1)} %pad_maximum_fusion.9), channel_id=1, source_target_pairs={{0,192},{1,25},{8,200},{9,17},{16,208},{17,9},{24,216},{25,1},{64,... | collective-permute-start | bytes 3145736 | tf_op jit(solution)/shard_map/ppermute | solution.py:28
  188.6 9.5 %collective-permute-start.24 = (bf16[64,2048]{1,0:T(8,128)(2,1)S(1)}, bf16[64,2048]{1,0:T(8,128)(2,1)S(1)}, u32[]{:S(2)}, u32[]{:S(2)}) collective-permute-start(bf16[64,2048]{1,0:T(8,128)(2,1)S(1)} %get-tuple-element.45), channel_id=1, source_target_pairs={{0,24},{1,193},{8,16},{9,201},{16,8},{17,209},{24,0},{25,217},{64,... | collective-permute-start | bytes 786440 | tf_op jit(solution)/shard_map/ppermute | solution.py:28
  189.8 8.4 %collective-permute-start.23 = (bf16[64,2048]{1,0:T(8,128)(2,1)S(1)}, bf16[64,2048]{1,0:T(8,128)(2,1)S(1)}, u32[]{:S(2)}, u32[]{:S(2)}) collective-permute-start(bf16[64,2048]{1,0:T(8,128)(2,1)S(1)} %get-tuple-element.46), channel_id=1, source_target_pairs={{0,16},{1,129},{8,24},{9,137},{16,0},{17,145},{24,8},{25,153},{64,... | collective-permute-start | bytes 786440 | tf_op jit(solution)/shard_map/ppermute | solution.py:28
  198.3 17.7 %collective-permute-start.26 = (bf16[64,1024]{1,0:T(8,128)(2,1)S(1)}, bf16[64,1024]{1,0:T(8,128)(2,1)S(1)}, u32[]{:S(2)}, u32[]{:S(2)}) collective-permute-start(bf16[64,1024]{1,0:T(8,128)(2,1)S(1)} %get-tuple-element.12), channel_id=1, source_target_pairs={{32,0},{1,33},{0,1},{33,32},{34,2},{3,35},{2,3},{35,34},{36,4},{5,... | collective-permute-start | bytes 393224 | tf_op jit(solution)/shard_map/ppermute | solution.py:137
  198.6 17.4 %collective-permute-start.25 = (bf16[64,1024]{1,0:T(8,128)(2,1)S(1)}, bf16[64,1024]{1,0:T(8,128)(2,1)S(1)}, u32[]{:S(2)}, u32[]{:S(2)}) collective-permute-start(bf16[64,1024]{1,0:T(8,128)(2,1)S(1)} %get-tuple-element.13), channel_id=1, source_target_pairs={{1,32},{32,1},{3,34},{34,3},{5,36},{36,5},{7,38},{38,7},{9,40},{40... | collective-permute-start | bytes 393224 | tf_op jit(solution)/shard_map/ppermute | solution.py:138
  (9 other events, 48.4 us)

commit v3 on v1

v3 whole, which is shorter than its diff:
```python
import jax
import jax.numpy as jnp
from jax import lax
from jax.experimental.layout import Layout, with_layout_constraint
from jax.sharding import Mesh
from jax.sharding import PartitionSpec as P

AXES = ("y", "zh", "x", "zl", "c")
ORDER = (0, 1, 3, 2)
BF16 = jnp.bfloat16
F32 = jnp.float32


def xor_perm(n, k):
    return [(i, i ^ k) for i in range(n)]


def plane_perm(k, x_core):
    pairs = []
    for y in range(4):
        for x in range(4):
            for c in range(2):
                y2, x2 = (y, x ^ k) if c == x_core else (y ^ k, x)
                pairs.append(((y * 4 + x) * 2 + c, (y2 * 4 + x2) * 2 + c))
    return pairs


def send_plane(value, k, x_core):
    return lax.ppermute(value, ("y", "x", "c"), plane_perm(k, x_core))


def pick(value, index):
    return lax.dynamic_index_in_dim(value, index, 0, keepdims=False)


def xor_rows(value, index):
    return jnp.stack([pick(value, index ^ k) for k in ORDER])


def on_device(tokens, gate_up, cotangent):
    rows, feats = tokens.shape
    half = gate_up.shape[2]
    y, zh, x, zl, c = (lax.axis_index(a) for a in AXES)
    shift = y ^ zl
    same = zh == c
    core0 = c == 0
    fwd_a, fwd_b = [(0, 2), (3, 1), (1, 0), (2, 3)], [(1, 2), (2, 1)]
    back_a = [(b, a) for a, b in fwd_a]

    recv_a = lax.ppermute(tokens, ("zh", "c"), fwd_a)
    recv_b = lax.ppermute(tokens, ("zh", "c"), fwd_b)
    own = jnp.where(same, tokens, recv_a)
    sib = jnp.where(same, recv_a, recv_b)
    block = jnp.concatenate([own, sib], axis=1)

    w_own = gate_up.reshape(feats, 2 * half)
    w_sib = lax.ppermute(w_own, "c", xor_perm(2, 1))
    weights = jnp.concatenate([w_own, w_sib], axis=0)

    part = jnp.stack([block] + [send_plane(block, k, 0) for k in ORDER[1:]])
    size = rows
    cot = xor_rows(cotangent.reshape(4, rows, half), x)

    near, far = send_plane(part, 1, 1), send_plane(part, 3, 1)
    relay = [send_plane(near[:2], 3, 1), send_plane(far[2:], 1, 1)]

    def rows_of(blocks):
        return jnp.concatenate(blocks).reshape(-1, 2 * feats)

    first = lax.optimization_barrier(rows_of([part, near, far]))
    head = jnp.dot(first, weights, preferred_element_type=F32)
    head, *relay = lax.optimization_barrier((head, *relay))
    last = rows_of(relay)
    pre = jnp.concatenate([head, jnp.dot(last, weights, preferred_element_type=F32)])
    pre = pre.reshape(4, 4, size, 2 * half)

    def slab(k):
        place = shift ^ k
        place = place ^ (place >> 1)
        major = lax.dynamic_index_in_dim(pre, place, 0, keepdims=False)
        minor = lax.dynamic_index_in_dim(pre, place, 1, keepdims=False)
        return jnp.where(core0, major, minor)

    total = slab(0)
    for k in (1, 2, 3):
        total = total + lax.ppermute(
            slab(k).astype(BF16), "zl", xor_perm(4, k)
        ).astype(F32)
    gate_pre, up_pre = total[..., :half], total[..., half:]
    sigmoid = jax.nn.sigmoid(gate_pre)
    activated = gate_pre * sigmoid
    hidden = (activated * up_pre).astype(BF16)
    grad_out = cot.astype(F32)
    grad_gate = grad_out * up_pre * sigmoid * (1.0 + gate_pre * (1.0 - sigmoid))
    grad_up = grad_out * activated
    grads = jnp.concatenate([grad_gate, grad_up], axis=-1).astype(BF16)

    gathered = jnp.stack(
        [grads] + [lax.ppermute(grads, "zl", xor_perm(4, k)) for k in (1, 2, 3)]
    )
    ordered = xor_rows(gathered, shift)
    ordered = jnp.where(core0, ordered, jnp.swapaxes(ordered, 0, 1))
    g_flat = ordered.reshape(16 * size, 2 * half)

    def back(v):
        out = lax.dot_general(
            v, weights, (((1,), (1,)), ((), ())), preferred_element_type=F32
        )
        return out.reshape(-1, 4, size, 2 * feats)

    cut = 12 * size
    (relay,) = back(g_flat[cut:])
    relay = relay.astype(BF16)
    low, high = send_plane(relay[:2], 1, 1), send_plane(relay[2:], 3, 1)
    out, near, far = back(g_flat[:cut])
    far = jnp.concatenate([far[:2] + low.astype(F32), far[2:]]).astype(BF16)
    near = jnp.concatenate([near[:2], near[2:] + high.astype(F32)]).astype(BF16)
    recv = [send_plane(near, 1, 1), send_plane(far, 3, 1)]
    t_sib = jnp.concatenate([first[:, feats:], last[:, feats:]])
    t_sib = lax.ppermute(t_sib, "c", xor_perm(2, 1))
    g_sib = lax.ppermute(g_flat, "c", xor_perm(2, 1))
    weight_grad = lax.dot_general(
        jnp.concatenate([first[:, :feats], last[:, :feats], t_sib]),
        jnp.concatenate([g_flat, g_sib]),
        (((0,), (0,)), ((), ())),
        preferred_element_type=F32,
    )
    weight_grad = weight_grad.astype(BF16)
    *recv, weight_grad = lax.optimization_barrier((*recv, weight_grad))
    out = out + recv[0].astype(F32) + recv[1].astype(F32)
    part = out[0]
    recv = [send_plane(out[i].astype(BF16), ORDER[i], 0) for i in (1, 2, 3)]
    weight_grad = weight_grad.reshape(feats, 2, half)
    weight_grad = with_layout_constraint(weight_grad, Layout((0, 1, 2)))
    *recv, weight_grad = lax.optimization_barrier((*recv, weight_grad))
    for v in recv:
        part = part + v.astype(F32)
    out = part
    g_own, g_sib = out[:, :feats].astype(BF16), out[:, feats:].astype(BF16)
    recv_a = lax.ppermute(jnp.where(same, g_sib, g_own), ("zh", "c"), back_a)
    recv_b = lax.ppermute(g_sib, ("zh", "c"), fwd_b)
    first = jnp.where(same, out[:, :feats], recv_b.astype(F32))
    input_grad = (first + recv_a.astype(F32)).astype(BF16)

    places = [(x ^ k) ^ ((x ^ k) >> 1) for k in range(4)]
    hidden = jnp.stack([pick(hidden, p) for p in places]).reshape(4 * rows, half)
    return hidden, input_grad, weight_grad


def solution(mesh):
    split = Mesh(mesh.devices.reshape(4, 2, 4, 4, 2), AXES)
    row, col = ("y", "zh", "x"), ("zl", "c")
    in_specs = (P(row, col), P(col, None, row), P(col, row))
    out_specs = (P(col, row), P(row, col), P(col, None, row))
    return jax.shard_map(
        on_device, mesh=split, in_specs=in_specs, out_specs=out_specs, check_vma=False
    )
```

time: 234 us -> 213 us (0.910)
  waiting for transfers between devices: 126 us -> 93.1 us
  local copies, waits for them, and re-layouts: 12 us -> 19.5 us
  starting transfers between devices: 69.2 us -> 74 us
    ppermute x12 -> x14, waiting for transfers between devices: 52.7 us -> 29.7 us  [send_plane(): return lax.ppermute(value, ('y', 'x', 'c'), plane_perm(k, x_core))]
    ppermute x2, starting transfers between devices: 2.73 us -> 8.39 us  [the longest x1 4.96 us: on_device(): g_sib = lax.ppermute(g_flat, 'c', xor_perm(2, 1))]
    ppermute x3, waiting for transfers between devices: 34.7 us -> 30.1 us  [on_device(): lax.ppermute(slab(k).astype(BF16), 'zl', xor_perm(4, k)).astype(F32)]
    reshape x0 -> x1, local copies, waits for them, and re-layouts: none -> 4.48 us  [on_device(): weight_grad = weight_grad.reshape(feats, 2, half)]
    ppermute x3, waiting for transfers between devices: 33 us -> 29.3 us  [on_device(): lax.ppermute(grads, 'zl', xor_perm(4, k))]
    ppermute x1, starting transfers between devices: 3.33 us -> 0.09 us  [on_device(): w_sib = lax.ppermute(w_own, 'c', xor_perm(2, 1))]
    ppermute x1, starting transfers between devices: 0.11 us -> 3.33 us  [on_device(): recv_a = lax.ppermute(tokens, ('zh', 'c'), fwd_a)]
    another operation x7 -> x8, other arithmetic: 5.41 us -> 3.08 us  [the longest x2 3.25 us: on_device(): plane = jnp.stack([part] + [send_plane(part, k, 1) for k in (1, 2, 3)])]
  transfers between devices with their start and end apart: 25 -> 27, of which waited for: 17 -> 16; matrix products, arithmetic and copies ran while one was open for 3% -> 16% of each run, Pallas kernels for 0% -> 0%
where the time goes in v3:
time: 213 us
  waiting for transfers between devices  93.1 us (44%)
  starting transfers between devices  74 us (35%)
  local copies, waits for them, and re-layouts  19.5 us (9%)
  matrix products  17 us (8%)
  other arithmetic  8.1 us (4%)
    ppermute x3, waiting for transfers between devices, on_device(): lax.ppermute(slab(k).astype(BF16), 'zl', xor_perm(4, k)).astype(F32)  30.1 us
    ppermute x14, waiting for transfers between devices, send_plane(): return lax.ppermute(value, ('y', 'x', 'c'), plane_perm(k, x_core))  29.7 us
    ppermute x3, waiting for transfers between devices, on_device(): lax.ppermute(grads, 'zl', xor_perm(4, k))  29.3 us
    ppermute x3, starting transfers between devices, on_device(): lax.ppermute(grads, 'zl', xor_perm(4, k))  24.2 us
    ppermute x14, starting transfers between devices, send_plane(): return lax.ppermute(value, ('y', 'x', 'c'), plane_perm(k, x_core))  14.4 us
    ppermute x1, starting transfers between devices, on_device(): recv_b = lax.ppermute(g_sib, ('zh', 'c'), fwd_b)  12.9 us
    unnamed x22, local copies, waits for them, and re-layouts  7.79 us
    dot_general x1, matrix products, on_device(): lax.dot_general(jnp.concatenate([first[:, :feats], last[:, :feats], t_sib...  7.53 us
  transfers between devices with their start and end apart: 27, of which 16 were waited for; matrix products, arithmetic and copies ran while one was open for 16% of the time, Pallas kernels for 0%

profile of v3, /device:TPU:1, one launch (start us, length us, event | category | flops | bytes accessed | tf_op | source)
XLA Modules:
  0.0 212.8 jit_solution(13431446248409924991)
XLA Ops:
  0.6 3.3 %collective-permute-start = (bf16[64,1024]{1,0:T(8,128)(2,1)}, bf16[64,1024]{1,0:T(8,128)(2,1)S(1)}, u32[]{:S(2)}, u32[]{:S(2)}) collective-permute-start(bf16[64,1024]{1,0:T(8,128)(2,1)} %param.3), channel_id=1, source_target_pairs={{0,32},{33,1},{1,0},{32,33},{2,34},{35,3},{3,2},{34,35},{4,36},{37... | collective-permute-start | bytes 393224 | tf_op jit(solution)/shard_map/ppermute | solution.py:50
  4.0 7.0 %collective-permute-start.1 = (bf16[64,1024]{1,0:T(8,128)(2,1)}, bf16[64,1024]{1,0:T(8,128)(2,1)S(1)}, u32[]{:S(2)}, u32[]{:S(2)}) collective-permute-start(bf16[64,1024]{1,0:T(8,128)(2,1)} %param.3), channel_id=1, source_target_pairs={{1,32},{32,1},{3,34},{34,3},{5,36},{36,5},{7,38},{38,7},{9,40},{40... | collective-permute-start | bytes 393224 | tf_op jit(solution)/shard_map/ppermute | solution.py:51
  11.0 2.1 %copy.10 = bf16[128,8,2,512]{3,1,2,0:T(8,128)(2,1)S(1)} copy(bf16[128,8,2,512]{3,2,1,0:T(2,128)(2,1)} %bitcast.107) | data formatting | bytes 4194304
  13.2 2.1 collective-permute-done.1
  16.1 2.7 %collective-permute-start.3 = (bf16[64,2048]{1,0:T(8,128)(2,1)}, bf16[64,2048]{1,0:T(8,128)(2,1)S(1)}, u32[]{:S(2)}, u32[]{:S(2)}) collective-permute-start(bf16[64,2048]{1,0:T(8,128)(2,1)} %get-tuple-element.59), channel_id=1, source_target_pairs={{0,24},{1,193},{8,16},{9,201},{16,8},{17,209},{24,0},{25,217},{64,... | collective-permute-start | bytes 786440 | tf_op jit(solution)/shard_map/ppermute | solution.py:29
  24.6 2.5 %collective-permute-done.4 = bf16[64,2048]{1,0:T(8,128)(2,1)S(1)} collective-permute-done((bf16[64,2048]{1,0:T(8,128)(2,1)}, bf16[64,2048]{1,0:T(8,128)(2,1)S(1)}, u32[]{:S(2)}, u32[]{:S(2)}) %collective-permute-start.4) | collective-permute-done | bytes 262176 | tf_op jit(solution)/shard_map/ppermute | solution.py:29
  27.2 2.6 %collective-permute-start.6 = (bf16[4,64,2048]{2,1,0:T(8,128)(2,1)S(1)}, bf16[4,64,2048]{2,1,0:T(8,128)(2,1)S(1)}, u32[]{:S(2)}, u32[]{:S(2)}) collective-permute-start(bf16[4,64,2048]{2,1,0:T(8,128)(2,1)S(1)} %pad_maximum_fusion.4), channel_id=1, source_target_pairs={{0,192},{1,25},{8,200},{9,17},{16,208},{17,9},{24,216},{25,1},{64,... | collective-permute-start | bytes 3145736 | tf_op jit(solution)/shard_map/ppermute | solution.py:29
  29.9 12.6 %collective-permute-done.6 = bf16[4,64,2048]{2,1,0:T(8,128)(2,1)S(1)} collective-permute-done((bf16[4,64,2048]{2,1,0:T(8,128)(2,1)S(1)}, bf16[4,64,2048]{2,1,0:T(8,128)(2,1)S(1)}, u32[]{:S(2)}, u32[]{:S(2)}) %collective-permute-start.6) | collective-permute-done | bytes 1048608 | tf_op jit(solution)/shard_map/ppermute | solution.py:29
  45.4 2.9 %constant_dynamic-update-slice_fusion.6 = bf16[2048,1024]{1,0:T(8,128)(2,1)S(1)} fusion(bf16[2048,1024]{1,0:T(8,128)(2,1)S(1)} %copy-done.3, bf16[1024,1024]{1,0:T(8,128)(2,1)} %collective-permute-done.7), kind=kLoop, calls=%fused_computation.69 | loop fusion | bytes 4194304 | tf_op jit(solution)/shard_map/concatenate | solution.py:58
  48.3 3.4 %fusion.43 = f32[768,1024]{1,0:T(8,128)S(1)} fusion(bf16[768,2048]{1,0:T(8,128)(2,1)S(1)} %bitcast.103, bf16[2048,1024]{1,0:T(8,128)(2,1)S(1)} %constant_dynamic-update-slice_fusion.6), kind=kOutput, calls=%fused_computation.92 | convolution fusion | flops 3221225472 | bytes 10485760 | tf_op jit(solution)/shard_map/dot_general | solution.py:71
  55.4 2.0 copy-done
  62.1 2.4 %fusion.38 = (bf16[768,1024]{1,0:T(8,128)(2,1)S(1)}, bf16[768,1024]{1,0:T(8,128)(2,1)S(1)}) fusion(bf16[768,2048]{1,0:T(8,128)(2,1)} %bitcast.104), kind=kLoop, calls=%fused_computation.87 | loop fusion | bytes 6291456 | tf_op jit(solution)/shard_map/slice | solution.py:123
  64.4 15.9 %collective-permute-done.10 = bf16[4,64,1024]{2,1,0:T(8,128)(2,1)S(1)} collective-permute-done((bf16[4,64,1024]{2,1,0:T(8,128)(2,1)}, bf16[4,64,1024]{2,1,0:T(8,128)(2,1)S(1)}, u32[]{:S(2)}, u32[]{:S(2)}) %collective-permute-start.10) | collective-permute-done | bytes 524320 | tf_op jit(solution)/shard_map/ppermute | solution.py:86
  80.8 13.8 %collective-permute-done.12 = bf16[4,64,1024]{2,1,0:T(8,128)(2,1)} collective-permute-done((bf16[4,64,1024]{2,1,0:T(8,128)(2,1)S(1)}, bf16[4,64,1024]{2,1,0:T(8,128)(2,1)}, u32[]{:S(2)}, u32[]{:S(2)}) %collective-permute-start.12) | collective-permute-done | bytes 524320 | tf_op jit(solution)/shard_map/ppermute | solution.py:86
  98.1 22.6 %collective-permute-start.14 = (bf16[4,64,1024]{2,1,0:T(8,128)(2,1)S(1)}, bf16[4,64,1024]{2,1,0:T(8,128)(2,1)S(1)}, u32[]{:S(2)}, u32[]{:S(2)}) collective-permute-start(bf16[4,64,1024]{2,1,0:T(8,128)(2,1)S(1)} %pad_maximum_fusion.8), channel_id=1, source_target_pairs={{0,4},{2,6},{4,0},{6,2},{1,5},{3,7},{5,1},{7,3},{8,12},{10,14},{12... | collective-permute-start | bytes 1572872 | tf_op jit(solution)/shard_map/ppermute | solution.py:99
  121.0 3.4 %collective-permute-start.20 = (bf16[1024,1024]{1,0:T(8,128)(2,1)S(1)}, bf16[1024,1024]{1,0:T(8,128)(2,1)S(1)}, u32[]{:S(2)}, u32[]{:S(2)}) collective-permute-start(bf16[1024,1024]{1,0:T(8,128)(2,1)S(1)} %pad_maximum_fusion.3), channel_id=1, source_target_pairs={{0,1},{1,0},{2,3},{3,2},{4,5},{5,4},{6,7},{7,6},{8,9},{9,8},{10,11... | collective-permute-start | bytes 6291464 | tf_op jit(solution)/shard_map/ppermute | solution.py:120
  124.5 29.3 %collective-permute-done.14 = bf16[4,64,1024]{2,1,0:T(8,128)(2,1)S(1)} collective-permute-done((bf16[4,64,1024]{2,1,0:T(8,128)(2,1)S(1)}, bf16[4,64,1024]{2,1,0:T(8,128)(2,1)S(1)}, u32[]{:S(2)}, u32[]{:S(2)}) %collective-permute-start.14) | collective-permute-done | bytes 524320 | tf_op jit(solution)/shard_map/ppermute | solution.py:99
  159.1 5.0 %collective-permute-start.21 = (bf16[1024,1024]{1,0:T(8,128)(2,1)S(1)}, bf16[1024,1024]{1,0:T(8,128)(2,1)}, u32[]{:S(2)}, u32[]{:S(2)}) collective-permute-start(bf16[1024,1024]{1,0:T(8,128)(2,1)S(1)} %bitcast.97), channel_id=1, source_target_pairs={{0,1},{1,0},{2,3},{3,2},{4,5},{5,4},{6,7},{7,6},{8,9},{9,8},{10,11... | collective-permute-start | bytes 6291464 | tf_op jit(solution)/shard_map/ppermute | solution.py:121
  164.1 3.4 %fusion.42 = (bf16[768,2048]{1,0:T(8,128)(2,1)S(1)}, f32[768,2048]{1,0:T(8,128)S(1)}) fusion(bf16[768,1024]{1,0:T(8,128)(2,1)S(1)} %bitcast.110, bf16[2048,1024]{1,0:T(8,128)(2,1)S(1)} %copy-done.5), kind=kOutput, calls=%fused_computation.91 | convolution fusion | flops 3222798336 | bytes 15204352 | tf_op jit(solution)/shard_map/dot_general | solution.py:106
  170.4 7.5 %fusion.14 = bf16[1024,1024]{1,0:T(8,128)(2,1)} fusion(bf16[1024,1024]{1,0:T(8,128)(2,1)} %collective-permute-done.21, bf16[1024,1024]{1,0:T(8,128)(2,1)S(1)} %bitcast.98, bf16[1024,1024]{1,0:T(8,128)(2,1)S(1)} %collective-permute-done.20, bf16[256,1024]{1,0:T(8,128)(2,1)S(1)} %get-tuple-element.45, bf16[768,1024]{1,0:T(8,128)(2,1)S(1)} %get-tuple-element.32), kind=kOutput, calls=%fused_computation.18 | convolution fusion | flops 4316987392 | bytes 10485760 | tf_op jit(solution)/shard_map/dot_general | solution.py:122
  178.0 4.5 %collective-permute-done.17 = bf16[4,64,2048]{2,1,0:T(8,128)(2,1)S(1)} collective-permute-done((bf16[4,64,2048]{2,1,0:T(8,128)(2,1)S(1)}, bf16[4,64,2048]{2,1,0:T(8,128)(2,1)S(1)}, u32[]{:S(2)}, u32[]{:S(2)}) %collective-permute-start.17) | collective-permute-done | bytes 1048608 | tf_op jit(solution)/shard_map/ppermute | solution.py:29
  186.4 2.2 %collective-permute-start.23 = (bf16[64,2048]{1,0:T(8,128)(2,1)}, bf16[64,2048]{1,0:T(8,128)(2,1)S(1)}, u32[]{:S(2)}, u32[]{:S(2)}) collective-permute-start(bf16[64,2048]{1,0:T(8,128)(2,1)} %get-tuple-element.43), channel_id=1, source_target_pairs={{0,24},{1,193},{8,16},{9,201},{16,8},{17,209},{24,0},{25,217},{64,... | collective-permute-start | bytes 786440 | tf_op jit(solution)/shard_map/ppermute | solution.py:29
  189.2 4.5 %reshape.88 = bf16[1024,2,512]{2,1,0:T(2,128)(2,1)} reshape(bf16[1024,1024]{1,0:T(8,128)(2,1)} %fusion.14) | data formatting | bytes 4194304 | tf_op jit(solution)/shard_map/reshape | solution.py:133
  196.6 12.9 %collective-permute-start.25 = (bf16[64,1024]{1,0:T(8,128)(2,1)S(1)}, bf16[64,1024]{1,0:T(8,128)(2,1)S(1)}, u32[]{:S(2)}, u32[]{:S(2)}) collective-permute-start(bf16[64,1024]{1,0:T(8,128)(2,1)S(1)} %get-tuple-element.24), channel_id=1, source_target_pairs={{1,32},{32,1},{3,34},{34,3},{5,36},{36,5},{7,38},{38,7},{9,40},{40... | collective-permute-start | bytes 393224 | tf_op jit(solution)/shard_map/ppermute | solution.py:141
  (97 shorter events, 41.1 us)
Async XLA Ops:
  0.6 12.6 %collective-permute-start = (bf16[64,1024]{1,0:T(8,128)(2,1)}, bf16[64,1024]{1,0:T(8,128)(2,1)S(1)}, u32[]{:S(2)}, u32[]{:S(2)}) collective-permute-start(bf16[64,1024]{1,0:T(8,128)(2,1)} %param.3), channel_id=1, source_target_pairs={{0,32},{33,1},{1,0},{32,33},{2,34},{35,3},{3,2},{34,35},{4,36},{37... | collective-permute-start | bytes 393224 | tf_op jit(solution)/shard_map/ppermute | solution.py:50
  4.0 11.3 %collective-permute-start.1 = (bf16[64,1024]{1,0:T(8,128)(2,1)}, bf16[64,1024]{1,0:T(8,128)(2,1)S(1)}, u32[]{:S(2)}, u32[]{:S(2)}) collective-permute-start(bf16[64,1024]{1,0:T(8,128)(2,1)} %param.3), channel_id=1, source_target_pairs={{1,32},{32,1},{3,34},{34,3},{5,36},{36,5},{7,38},{38,7},{9,40},{40... | collective-permute-start | bytes 393224 | tf_op jit(solution)/shard_map/ppermute | solution.py:51
  13.1 32.3 %collective-permute-start.7 = (bf16[1024,1024]{1,0:T(8,128)(2,1)S(1)}, bf16[1024,1024]{1,0:T(8,128)(2,1)}, u32[]{:S(2)}, u32[]{:S(2)}) collective-permute-start(bf16[1024,1024]{1,0:T(8,128)(2,1)S(1)} %bitcast.95), channel_id=1, source_target_pairs={{0,1},{1,0},{2,3},{3,2},{4,5},{5,4},{6,7},{7,6},{8,9},{9,8},{10,11... | collective-permute-start | bytes 6291464 | tf_op jit(solution)/shard_map/ppermute | solution.py:57
  18.8 8.3 %collective-permute-start.4 = (bf16[64,2048]{1,0:T(8,128)(2,1)}, bf16[64,2048]{1,0:T(8,128)(2,1)S(1)}, u32[]{:S(2)}, u32[]{:S(2)}) collective-permute-start(bf16[64,2048]{1,0:T(8,128)(2,1)} %get-tuple-element.59), channel_id=1, source_target_pairs={{0,16},{1,129},{8,24},{9,137},{16,0},{17,145},{24,8},{25,153},{64,... | collective-permute-start | bytes 786440 | tf_op jit(solution)/shard_map/ppermute | solution.py:29
  27.2 15.2 %collective-permute-start.6 = (bf16[4,64,2048]{2,1,0:T(8,128)(2,1)S(1)}, bf16[4,64,2048]{2,1,0:T(8,128)(2,1)S(1)}, u32[]{:S(2)}, u32[]{:S(2)}) collective-permute-start(bf16[4,64,2048]{2,1,0:T(8,128)(2,1)S(1)} %pad_maximum_fusion.4), channel_id=1, source_target_pairs={{0,192},{1,25},{8,200},{9,17},{16,208},{17,9},{24,216},{25,1},{64,... | collective-permute-start | bytes 3145736 | tf_op jit(solution)/shard_map/ppermute | solution.py:29
  29.8 13.9 %collective-permute-start.5 = (bf16[4,64,2048]{2,1,0:T(8,128)(2,1)S(1)}, bf16[4,64,2048]{2,1,0:T(8,128)(2,1)S(1)}, u32[]{:S(2)}, u32[]{:S(2)}) collective-permute-start(bf16[4,64,2048]{2,1,0:T(8,128)(2,1)S(1)} %pad_maximum_fusion.4), channel_id=1, source_target_pairs={{0,64},{1,9},{8,72},{9,1},{16,80},{17,25},{24,88},{25,17},{64,0},{... | collective-permute-start | bytes 3145736 | tf_op jit(solution)/shard_map/ppermute | solution.py:29
  42.5 9.2 %collective-permute-start.9 = (bf16[2,64,2048]{2,1,0:T(8,128)(2,1)S(1)}, bf16[2,64,2048]{2,1,0:T(8,128)(2,1)S(1)}, u32[]{:S(2)}, u32[]{:S(2)}) collective-permute-start(bf16[2,64,2048]{2,1,0:T(8,128)(2,1)S(1)} %slice.124), channel_id=1, source_target_pairs={{0,64},{1,9},{8,72},{9,1},{16,80},{17,25},{24,88},{25,17},{64,0},{... | collective-permute-start | bytes 1572872 | tf_op jit(solution)/shard_map/ppermute | solution.py:29
  43.8 9.6 %collective-permute-start.8 = (bf16[2,64,2048]{2,1,0:T(8,128)(2,1)S(1)}, bf16[2,64,2048]{2,1,0:T(8,128)(2,1)S(1)}, u32[]{:S(2)}, u32[]{:S(2)}) collective-permute-start(bf16[2,64,2048]{2,1,0:T(8,128)(2,1)S(1)} %slice.123), channel_id=1, source_target_pairs={{0,192},{1,25},{8,200},{9,17},{16,208},{17,9},{24,216},{25,1},{64,... | collective-permute-start | bytes 1572872 | tf_op jit(solution)/shard_map/ppermute | solution.py:29
  58.5 21.8 %collective-permute-start.10 = (bf16[4,64,1024]{2,1,0:T(8,128)(2,1)}, bf16[4,64,1024]{2,1,0:T(8,128)(2,1)S(1)}, u32[]{:S(2)}, u32[]{:S(2)}) collective-permute-start(bf16[4,64,1024]{2,1,0:T(8,128)(2,1)} %get-tuple-element.29), channel_id=1, source_target_pairs={{0,2},{2,0},{4,6},{6,4},{1,3},{3,1},{5,7},{7,5},{8,10},{10,8},{12,... | collective-permute-start | bytes 1572872 | tf_op jit(solution)/shard_map/ppermute | solution.py:86
  59.7 21.1 %collective-permute-start.11 = (bf16[4,64,1024]{2,1,0:T(8,128)(2,1)S(1)}, bf16[4,64,1024]{2,1,0:T(8,128)(2,1)S(1)}, u32[]{:S(2)}, u32[]{:S(2)}) collective-permute-start(bf16[4,64,1024]{2,1,0:T(8,128)(2,1)S(1)} %get-tuple-element.30), channel_id=1, source_target_pairs={{0,4},{2,6},{4,0},{6,2},{1,5},{3,7},{5,1},{7,3},{8,12},{10,14},{12... | collective-permute-start | bytes 1572872 | tf_op jit(solution)/shard_map/ppermute | solution.py:86
  60.9 33.7 %collective-permute-start.12 = (bf16[4,64,1024]{2,1,0:T(8,128)(2,1)S(1)}, bf16[4,64,1024]{2,1,0:T(8,128)(2,1)}, u32[]{:S(2)}, u32[]{:S(2)}) collective-permute-start(bf16[4,64,1024]{2,1,0:T(8,128)(2,1)S(1)} %get-tuple-element.31), channel_id=1, source_target_pairs={{0,6},{2,4},{4,2},{6,0},{1,7},{3,5},{5,3},{7,1},{8,14},{10,12},{12... | collective-permute-start | bytes 1572872 | tf_op jit(solution)/shard_map/ppermute | solution.py:86
  96.5 28.0 %collective-permute-start.15 = (bf16[4,64,1024]{2,1,0:T(8,128)(2,1)S(1)}, bf16[4,64,1024]{2,1,0:T(8,128)(2,1)S(1)}, u32[]{:S(2)}, u32[]{:S(2)}) collective-permute-start(bf16[4,64,1024]{2,1,0:T(8,128)(2,1)S(1)} %pad_maximum_fusion.8), channel_id=1, source_target_pairs={{0,6},{2,4},{4,2},{6,0},{1,7},{3,5},{5,3},{7,1},{8,14},{10,12},{12... | collective-permute-start | bytes 1572872 | tf_op jit(solution)/shard_map/ppermute | solution.py:99
  98.1 55.7 %collective-permute-start.14 = (bf16[4,64,1024]{2,1,0:T(8,128)(2,1)S(1)}, bf16[4,64,1024]{2,1,0:T(8,128)(2,1)S(1)}, u32[]{:S(2)}, u32[]{:S(2)}) collective-permute-start(bf16[4,64,1024]{2,1,0:T(8,128)(2,1)S(1)} %pad_maximum_fusion.8), channel_id=1, source_target_pairs={{0,4},{2,6},{4,0},{6,2},{1,5},{3,7},{5,1},{7,3},{8,12},{10,14},{12... | collective-permute-start | bytes 1572872 | tf_op jit(solution)/shard_map/ppermute | solution.py:99
  120.7 33.1 %collective-permute-start.13 = (bf16[4,64,1024]{2,1,0:T(8,128)(2,1)S(1)}, bf16[4,64,1024]{2,1,0:T(8,128)(2,1)S(1)}, u32[]{:S(2)}, u32[]{:S(2)}) collective-permute-start(bf16[4,64,1024]{2,1,0:T(8,128)(2,1)S(1)} %pad_maximum_fusion.8), channel_id=1, source_target_pairs={{0,2},{2,0},{4,6},{6,4},{1,3},{3,1},{5,7},{7,5},{8,10},{10,8},{12,... | collective-permute-start | bytes 1572872 | tf_op jit(solution)/shard_map/ppermute | solution.py:99
  121.0 49.4 %collective-permute-start.20 = (bf16[1024,1024]{1,0:T(8,128)(2,1)S(1)}, bf16[1024,1024]{1,0:T(8,128)(2,1)S(1)}, u32[]{:S(2)}, u32[]{:S(2)}) collective-permute-start(bf16[1024,1024]{1,0:T(8,128)(2,1)S(1)} %pad_maximum_fusion.3), channel_id=1, source_target_pairs={{0,1},{1,0},{2,3},{3,2},{4,5},{5,4},{6,7},{7,6},{8,9},{9,8},{10,11... | collective-permute-start | bytes 6291464 | tf_op jit(solution)/shard_map/ppermute | solution.py:120
  158.2 10.4 %collective-permute-start.18 = (bf16[2,64,2048]{2,1,0:T(8,128)(2,1)S(1)}, bf16[2,64,2048]{2,1,0:T(8,128)(2,1)S(1)}, u32[]{:S(2)}, u32[]{:S(2)}) collective-permute-start(bf16[2,64,2048]{2,1,0:T(8,128)(2,1)S(1)} %get-tuple-element.47), channel_id=1, source_target_pairs={{0,64},{1,9},{8,72},{9,1},{16,80},{17,25},{24,88},{25,17},{64,0},{... | collective-permute-start | bytes 1572872 | tf_op jit(solution)/shard_map/ppermute | solution.py:29
  158.4 9.6 %collective-permute-start.16 = (bf16[2,64,2048]{2,1,0:T(8,128)(2,1)S(1)}, bf16[2,64,2048]{2,1,0:T(8,128)(2,1)S(1)}, u32[]{:S(2)}, u32[]{:S(2)}) collective-permute-start(bf16[2,64,2048]{2,1,0:T(8,128)(2,1)S(1)} %get-tuple-element.48), channel_id=1, source_target_pairs={{0,192},{1,25},{8,200},{9,17},{16,208},{17,9},{24,216},{25,1},{64,... | collective-permute-start | bytes 1572872 | tf_op jit(solution)/shard_map/ppermute | solution.py:29
  159.1 11.3 %collective-permute-start.21 = (bf16[1024,1024]{1,0:T(8,128)(2,1)S(1)}, bf16[1024,1024]{1,0:T(8,128)(2,1)}, u32[]{:S(2)}, u32[]{:S(2)}) collective-permute-start(bf16[1024,1024]{1,0:T(8,128)(2,1)S(1)} %bitcast.97), channel_id=1, source_target_pairs={{0,1},{1,0},{2,3},{3,2},{4,5},{5,4},{6,7},{7,6},{8,9},{9,8},{10,11... | collective-permute-start | bytes 6291464 | tf_op jit(solution)/shard_map/ppermute | solution.py:121
  168.2 14.3 %collective-permute-start.17 = (bf16[4,64,2048]{2,1,0:T(8,128)(2,1)S(1)}, bf16[4,64,2048]{2,1,0:T(8,128)(2,1)S(1)}, u32[]{:S(2)}, u32[]{:S(2)}) collective-permute-start(bf16[4,64,2048]{2,1,0:T(8,128)(2,1)S(1)} %pad_maximum_fusion.6), channel_id=1, source_target_pairs={{0,64},{1,9},{8,72},{9,1},{16,80},{17,25},{24,88},{25,17},{64,0},{... | collective-permute-start | bytes 3145736 | tf_op jit(solution)/shard_map/ppermute | solution.py:29
  168.9 15.2 %collective-permute-start.19 = (bf16[4,64,2048]{2,1,0:T(8,128)(2,1)S(1)}, bf16[4,64,2048]{2,1,0:T(8,128)(2,1)S(1)}, u32[]{:S(2)}, u32[]{:S(2)}) collective-permute-start(bf16[4,64,2048]{2,1,0:T(8,128)(2,1)S(1)} %pad_maximum_fusion.7), channel_id=1, source_target_pairs={{0,192},{1,25},{8,200},{9,17},{16,208},{17,9},{24,216},{25,1},{64,... | collective-permute-start | bytes 3145736 | tf_op jit(solution)/shard_map/ppermute | solution.py:29
  185.6 8.1 %collective-permute-start.24 = (bf16[64,2048]{1,0:T(8,128)(2,1)}, bf16[64,2048]{1,0:T(8,128)(2,1)S(1)}, u32[]{:S(2)}, u32[]{:S(2)}) collective-permute-start(bf16[64,2048]{1,0:T(8,128)(2,1)} %get-tuple-element.42), channel_id=1, source_target_pairs={{0,16},{1,129},{8,24},{9,137},{16,0},{17,145},{24,8},{25,153},{64,... | collective-permute-start | bytes 786440 | tf_op jit(solution)/shard_map/ppermute | solution.py:29
  186.4 8.9 %collective-permute-start.23 = (bf16[64,2048]{1,0:T(8,128)(2,1)}, bf16[64,2048]{1,0:T(8,128)(2,1)S(1)}, u32[]{:S(2)}, u32[]{:S(2)}) collective-permute-start(bf16[64,2048]{1,0:T(8,128)(2,1)} %get-tuple-element.43), channel_id=1, source_target_pairs={{0,24},{1,193},{8,16},{9,201},{16,8},{17,209},{24,0},{25,217},{64,... | collective-permute-start | bytes 786440 | tf_op jit(solution)/shard_map/ppermute | solution.py:29
  196.5 13.8 %collective-permute-start.26 = (bf16[64,1024]{1,0:T(8,128)(2,1)S(1)}, bf16[64,1024]{1,0:T(8,128)(2,1)S(1)}, u32[]{:S(2)}, u32[]{:S(2)}) collective-permute-start(bf16[64,1024]{1,0:T(8,128)(2,1)S(1)} %get-tuple-element.23), channel_id=1, source_target_pairs={{32,0},{1,33},{0,1},{33,32},{34,2},{3,35},{2,3},{35,34},{36,4},{5,... | collective-permute-start | bytes 393224 | tf_op jit(solution)/shard_map/ppermute | solution.py:140
  196.6 15.5 %collective-permute-start.25 = (bf16[64,1024]{1,0:T(8,128)(2,1)S(1)}, bf16[64,1024]{1,0:T(8,128)(2,1)S(1)}, u32[]{:S(2)}, u32[]{:S(2)}) collective-permute-start(bf16[64,1024]{1,0:T(8,128)(2,1)S(1)} %get-tuple-element.24), channel_id=1, source_target_pairs={{1,32},{32,1},{3,34},{34,3},{5,36},{36,5},{7,38},{38,7},{9,40},{40... | collective-permute-start | bytes 393224 | tf_op jit(solution)/shard_map/ppermute | solution.py:141
  (11 other events, 105.5 us)

commit v4 on v3

--- a/solution.py
+++ b/solution.py
@@ -81,11 +81,11 @@
         minor = lax.dynamic_index_in_dim(pre, place, 1, keepdims=False)
         return jnp.where(core0, major, minor)
 
-    total = slab(0)
-    for k in (1, 2, 3):
-        total = total + lax.ppermute(
-            slab(k).astype(BF16), "zl", xor_perm(4, k)
-        ).astype(F32)
+    total, *sends = lax.optimization_barrier(
+        (slab(0), *(slab(k).astype(BF16) for k in (1, 2, 3)))
+    )
+    for k, send in zip((1, 2, 3), sends):
+        total = total + lax.ppermute(send, "zl", xor_perm(4, k)).astype(F32)
     gate_pre, up_pre = total[..., :half], total[..., half:]
     sigmoid = jax.nn.sigmoid(gate_pre)
     activated = gate_pre * sigmoid

time: 213 us -> 212 us (level)
  local copies, waits for them, and re-layouts: 19.5 us -> 17.3 us
    unnamed x22 -> x18, local copies, waits for them, and re-layouts: 7.79 us -> 5.78 us
where the time goes in v4:
time: 212 us; the launch traced here: 211 us
  waiting for transfers between devices  93.3 us (44%)
  starting transfers between devices  74 us (35%)
  local copies, waits for them, and re-layouts  17.3 us (8%)
  matrix products  16.9 us (8%)
  other arithmetic  8.44 us (4%)
    ppermute x3, waiting for transfers between devices, on_device(): total = total + lax.ppermute(send, 'zl', xor_perm(4, k)).astype(F32)  30.3 us
    ppermute x14, waiting for transfers between devices, send_plane(): return lax.ppermute(value, ('y', 'x', 'c'), plane_perm(k, x_core))  29.8 us
    ppermute x3, waiting for transfers between devices, on_device(): lax.ppermute(grads, 'zl', xor_perm(4, k))  29.3 us
    ppermute x3, starting transfers between devices, on_device(): lax.ppermute(grads, 'zl', xor_perm(4, k))  24.2 us
    ppermute x14, starting transfers between devices, send_plane(): return lax.ppermute(value, ('y', 'x', 'c'), plane_perm(k, x_core))  14.4 us
    ppermute x1, starting transfers between devices, on_device(): recv_b = lax.ppermute(g_sib, ('zh', 'c'), fwd_b)  12.6 us
    dot_general x1, matrix products, on_device(): lax.dot_general(jnp.concatenate([first[:, :feats], last[:, :feats], t_sib...  7.52 us
    ppermute x1, starting transfers between devices, on_device(): recv_b = lax.ppermute(tokens, ('zh', 'c'), fwd_b)  6.98 us
  transfers between devices with their start and end apart: 27, of which 16 were waited for; matrix products, arithmetic and copies ran while one was open for 16% of the time, Pallas kernels for 0%

profile of v4, /device:TPU:1, one launch (start us, length us, event | category | flops | bytes accessed | tf_op | source)
XLA Modules:
  0.0 211.2 jit_solution(4707545824587098055)
XLA Ops:
  0.6 3.3 %collective-permute-start = (bf16[64,1024]{1,0:T(8,128)(2,1)}, bf16[64,1024]{1,0:T(8,128)(2,1)S(1)}, u32[]{:S(2)}, u32[]{:S(2)}) collective-permute-start(bf16[64,1024]{1,0:T(8,128)(2,1)} %param.3), channel_id=1, source_target_pairs={{0,32},{33,1},{1,0},{32,33},{2,34},{35,3},{3,2},{34,35},{4,36},{37... | collective-permute-start | bytes 393224 | tf_op jit(solution)/shard_map/ppermute | solution.py:50
  4.0 7.0 %collective-permute-start.1 = (bf16[64,1024]{1,0:T(8,128)(2,1)}, bf16[64,1024]{1,0:T(8,128)(2,1)S(1)}, u32[]{:S(2)}, u32[]{:S(2)}) collective-permute-start(bf16[64,1024]{1,0:T(8,128)(2,1)} %param.3), channel_id=1, source_target_pairs={{1,32},{32,1},{3,34},{34,3},{5,36},{36,5},{7,38},{38,7},{9,40},{40... | collective-permute-start | bytes 393224 | tf_op jit(solution)/shard_map/ppermute | solution.py:51
  11.0 2.1 %copy.10 = bf16[128,8,2,512]{3,1,2,0:T(8,128)(2,1)S(1)} copy(bf16[128,8,2,512]{3,2,1,0:T(2,128)(2,1)} %bitcast.101) | data formatting | bytes 4194304
  13.2 2.1 collective-permute-done.1
  16.1 2.7 %collective-permute-start.3 = (bf16[64,2048]{1,0:T(8,128)(2,1)}, bf16[64,2048]{1,0:T(8,128)(2,1)S(1)}, u32[]{:S(2)}, u32[]{:S(2)}) collective-permute-start(bf16[64,2048]{1,0:T(8,128)(2,1)} %get-tuple-element.67), channel_id=1, source_target_pairs={{0,24},{1,193},{8,16},{9,201},{16,8},{17,209},{24,0},{25,217},{64,... | collective-permute-start | bytes 786440 | tf_op jit(solution)/shard_map/ppermute | solution.py:29
  24.6 2.5 %collective-permute-done.4 = bf16[64,2048]{1,0:T(8,128)(2,1)S(1)} collective-permute-done((bf16[64,2048]{1,0:T(8,128)(2,1)}, bf16[64,2048]{1,0:T(8,128)(2,1)S(1)}, u32[]{:S(2)}, u32[]{:S(2)}) %collective-permute-start.4) | collective-permute-done | bytes 262176 | tf_op jit(solution)/shard_map/ppermute | solution.py:29
  27.2 2.6 %collective-permute-start.6 = (bf16[4,64,2048]{2,1,0:T(8,128)(2,1)S(1)}, bf16[4,64,2048]{2,1,0:T(8,128)(2,1)S(1)}, u32[]{:S(2)}, u32[]{:S(2)}) collective-permute-start(bf16[4,64,2048]{2,1,0:T(8,128)(2,1)S(1)} %pad_maximum_fusion.4), channel_id=1, source_target_pairs={{0,192},{1,25},{8,200},{9,17},{16,208},{17,9},{24,216},{25,1},{64,... | collective-permute-start | bytes 3145736 | tf_op jit(solution)/shard_map/ppermute | solution.py:29
  29.9 12.6 %collective-permute-done.6 = bf16[4,64,2048]{2,1,0:T(8,128)(2,1)S(1)} collective-permute-done((bf16[4,64,2048]{2,1,0:T(8,128)(2,1)S(1)}, bf16[4,64,2048]{2,1,0:T(8,128)(2,1)S(1)}, u32[]{:S(2)}, u32[]{:S(2)}) %collective-permute-start.6) | collective-permute-done | bytes 1048608 | tf_op jit(solution)/shard_map/ppermute | solution.py:29
  45.4 2.9 %constant_dynamic-update-slice_fusion.6 = bf16[2048,1024]{1,0:T(8,128)(2,1)S(1)} fusion(bf16[2048,1024]{1,0:T(8,128)(2,1)S(1)} %copy-done.1, bf16[1024,1024]{1,0:T(8,128)(2,1)} %collective-permute-done.7), kind=kLoop, calls=%fused_computation.67 | loop fusion | bytes 4194304 | tf_op jit(solution)/shard_map/concatenate | solution.py:58
  48.3 3.4 %fusion.40 = f32[768,1024]{1,0:T(8,128)S(1)} fusion(bf16[768,2048]{1,0:T(8,128)(2,1)S(1)} %bitcast.97, bf16[2048,1024]{1,0:T(8,128)(2,1)S(1)} %constant_dynamic-update-slice_fusion.6), kind=kOutput, calls=%fused_computation.90 | convolution fusion | flops 3221225472 | bytes 10485760 | tf_op jit(solution)/shard_map/dot_general | solution.py:71
  60.2 2.2 %fusion.35 = (bf16[768,1024]{1,0:T(8,128)(2,1)S(1)}, bf16[768,1024]{1,0:T(8,128)(2,1)S(1)}) fusion(bf16[768,2048]{1,0:T(8,128)(2,1)} %bitcast.98), kind=kLoop, calls=%fused_computation.85 | loop fusion | bytes 6291456 | tf_op jit(solution)/shard_map/slice | solution.py:123
  62.4 16.2 %collective-permute-done.10 = bf16[4,64,1024]{2,1,0:T(8,128)(2,1)} collective-permute-done((bf16[4,64,1024]{2,1,0:T(8,128)(2,1)}, bf16[4,64,1024]{2,1,0:T(8,128)(2,1)}, u32[]{:S(2)}, u32[]{:S(2)}) %collective-permute-start.10) | collective-permute-done | bytes 524320 | tf_op jit(solution)/shard_map/ppermute | solution.py:88
  78.9 13.8 %collective-permute-done.12 = bf16[4,64,1024]{2,1,0:T(8,128)(2,1)} collective-permute-done((bf16[4,64,1024]{2,1,0:T(8,128)(2,1)S(1)}, bf16[4,64,1024]{2,1,0:T(8,128)(2,1)}, u32[]{:S(2)}, u32[]{:S(2)}) %collective-permute-start.12) | collective-permute-done | bytes 524320 | tf_op jit(solution)/shard_map/ppermute | solution.py:88
  96.5 22.6 %collective-permute-start.14 = (bf16[4,64,1024]{2,1,0:T(8,128)(2,1)S(1)}, bf16[4,64,1024]{2,1,0:T(8,128)(2,1)S(1)}, u32[]{:S(2)}, u32[]{:S(2)}) collective-permute-start(bf16[4,64,1024]{2,1,0:T(8,128)(2,1)S(1)} %pad_maximum_fusion.8), channel_id=1, source_target_pairs={{0,4},{2,6},{4,0},{6,2},{1,5},{3,7},{5,1},{7,3},{8,12},{10,14},{12... | collective-permute-start | bytes 1572872 | tf_op jit(solution)/shard_map/ppermute | solution.py:99
  119.3 3.4 %collective-permute-start.20 = (bf16[1024,1024]{1,0:T(8,128)(2,1)S(1)}, bf16[1024,1024]{1,0:T(8,128)(2,1)S(1)}, u32[]{:S(2)}, u32[]{:S(2)}) collective-permute-start(bf16[1024,1024]{1,0:T(8,128)(2,1)S(1)} %pad_maximum_fusion.3), channel_id=1, source_target_pairs={{0,1},{1,0},{2,3},{3,2},{4,5},{5,4},{6,7},{7,6},{8,9},{9,8},{10,11... | collective-permute-start | bytes 6291464 | tf_op jit(solution)/shard_map/ppermute | solution.py:120
  122.8 29.3 %collective-permute-done.14 = bf16[4,64,1024]{2,1,0:T(8,128)(2,1)S(1)} collective-permute-done((bf16[4,64,1024]{2,1,0:T(8,128)(2,1)S(1)}, bf16[4,64,1024]{2,1,0:T(8,128)(2,1)S(1)}, u32[]{:S(2)}, u32[]{:S(2)}) %collective-permute-start.14) | collective-permute-done | bytes 524320 | tf_op jit(solution)/shard_map/ppermute | solution.py:99
  153.1 2.0 copy-done.3
  157.5 5.0 %collective-permute-start.21 = (bf16[1024,1024]{1,0:T(8,128)(2,1)S(1)}, bf16[1024,1024]{1,0:T(8,128)(2,1)}, u32[]{:S(2)}, u32[]{:S(2)}) collective-permute-start(bf16[1024,1024]{1,0:T(8,128)(2,1)S(1)} %bitcast.91), channel_id=1, source_target_pairs={{0,1},{1,0},{2,3},{3,2},{4,5},{5,4},{6,7},{7,6},{8,9},{9,8},{10,11... | collective-permute-start | bytes 6291464 | tf_op jit(solution)/shard_map/ppermute | solution.py:121
  162.4 3.4 %fusion.39 = (bf16[768,2048]{1,0:T(8,128)(2,1)S(1)}, f32[768,2048]{1,0:T(8,128)S(1)}) fusion(bf16[768,1024]{1,0:T(8,128)(2,1)S(1)} %bitcast.104, bf16[2048,1024]{1,0:T(8,128)(2,1)S(1)} %copy-done.3), kind=kOutput, calls=%fused_computation.89 | convolution fusion | flops 3222798336 | bytes 15204352 | tf_op jit(solution)/shard_map/dot_general | solution.py:106
  168.8 7.5 %fusion.14 = bf16[1024,1024]{1,0:T(8,128)(2,1)} fusion(bf16[1024,1024]{1,0:T(8,128)(2,1)} %collective-permute-done.21, bf16[1024,1024]{1,0:T(8,128)(2,1)S(1)} %bitcast.92, bf16[1024,1024]{1,0:T(8,128)(2,1)S(1)} %collective-permute-done.20, bf16[256,1024]{1,0:T(8,128)(2,1)S(1)} %get-tuple-element.53, bf16[768,1024]{1,0:T(8,128)(2,1)S(1)} %get-tuple-element.40), kind=kOutput, calls=%fused_computation.18 | convolution fusion | flops 4316987392 | bytes 10485760 | tf_op jit(solution)/shard_map/dot_general | solution.py:122
  176.3 4.3 %collective-permute-done.17 = bf16[4,64,2048]{2,1,0:T(8,128)(2,1)S(1)} collective-permute-done((bf16[4,64,2048]{2,1,0:T(8,128)(2,1)S(1)}, bf16[4,64,2048]{2,1,0:T(8,128)(2,1)S(1)}, u32[]{:S(2)}, u32[]{:S(2)}) %collective-permute-start.17) | collective-permute-done | bytes 1048608 | tf_op jit(solution)/shard_map/ppermute | solution.py:29
  184.8 2.2 %collective-permute-start.23 = (bf16[64,2048]{1,0:T(8,128)(2,1)}, bf16[64,2048]{1,0:T(8,128)(2,1)S(1)}, u32[]{:S(2)}, u32[]{:S(2)}) collective-permute-start(bf16[64,2048]{1,0:T(8,128)(2,1)} %get-tuple-element.51), channel_id=1, source_target_pairs={{0,24},{1,193},{8,16},{9,201},{16,8},{17,209},{24,0},{25,217},{64,... | collective-permute-start | bytes 786440 | tf_op jit(solution)/shard_map/ppermute | solution.py:29
  187.5 4.5 %reshape.88 = bf16[1024,2,512]{2,1,0:T(2,128)(2,1)} reshape(bf16[1024,1024]{1,0:T(8,128)(2,1)} %fusion.14) | data formatting | bytes 4194304 | tf_op jit(solution)/shard_map/reshape | solution.py:133
  195.2 12.6 %collective-permute-start.25 = (bf16[64,1024]{1,0:T(8,128)(2,1)S(1)}, bf16[64,1024]{1,0:T(8,128)(2,1)S(1)}, u32[]{:S(2)}, u32[]{:S(2)}) collective-permute-start(bf16[64,1024]{1,0:T(8,128)(2,1)S(1)} %get-tuple-element.32), channel_id=1, source_target_pairs={{1,32},{32,1},{3,34},{34,3},{5,36},{36,5},{7,38},{38,7},{9,40},{40... | collective-permute-start | bytes 393224 | tf_op jit(solution)/shard_map/ppermute | solution.py:141
  (94 shorter events, 39.8 us)
Async XLA Ops:
  0.6 12.6 %collective-permute-start = (bf16[64,1024]{1,0:T(8,128)(2,1)}, bf16[64,1024]{1,0:T(8,128)(2,1)S(1)}, u32[]{:S(2)}, u32[]{:S(2)}) collective-permute-start(bf16[64,1024]{1,0:T(8,128)(2,1)} %param.3), channel_id=1, source_target_pairs={{0,32},{33,1},{1,0},{32,33},{2,34},{35,3},{3,2},{34,35},{4,36},{37... | collective-permute-start | bytes 393224 | tf_op jit(solution)/shard_map/ppermute | solution.py:50
  4.0 11.3 %collective-permute-start.1 = (bf16[64,1024]{1,0:T(8,128)(2,1)}, bf16[64,1024]{1,0:T(8,128)(2,1)S(1)}, u32[]{:S(2)}, u32[]{:S(2)}) collective-permute-start(bf16[64,1024]{1,0:T(8,128)(2,1)} %param.3), channel_id=1, source_target_pairs={{1,32},{32,1},{3,34},{34,3},{5,36},{36,5},{7,38},{38,7},{9,40},{40... | collective-permute-start | bytes 393224 | tf_op jit(solution)/shard_map/ppermute | solution.py:51
  13.1 32.3 %collective-permute-start.7 = (bf16[1024,1024]{1,0:T(8,128)(2,1)S(1)}, bf16[1024,1024]{1,0:T(8,128)(2,1)}, u32[]{:S(2)}, u32[]{:S(2)}) collective-permute-start(bf16[1024,1024]{1,0:T(8,128)(2,1)S(1)} %bitcast.89), channel_id=1, source_target_pairs={{0,1},{1,0},{2,3},{3,2},{4,5},{5,4},{6,7},{7,6},{8,9},{9,8},{10,11... | collective-permute-start | bytes 6291464 | tf_op jit(solution)/shard_map/ppermute | solution.py:57
  18.8 8.3 %collective-permute-start.4 = (bf16[64,2048]{1,0:T(8,128)(2,1)}, bf16[64,2048]{1,0:T(8,128)(2,1)S(1)}, u32[]{:S(2)}, u32[]{:S(2)}) collective-permute-start(bf16[64,2048]{1,0:T(8,128)(2,1)} %get-tuple-element.67), channel_id=1, source_target_pairs={{0,16},{1,129},{8,24},{9,137},{16,0},{17,145},{24,8},{25,153},{64,... | collective-permute-start | bytes 786440 | tf_op jit(solution)/shard_map/ppermute | solution.py:29
  27.2 15.2 %collective-permute-start.6 = (bf16[4,64,2048]{2,1,0:T(8,128)(2,1)S(1)}, bf16[4,64,2048]{2,1,0:T(8,128)(2,1)S(1)}, u32[]{:S(2)}, u32[]{:S(2)}) collective-permute-start(bf16[4,64,2048]{2,1,0:T(8,128)(2,1)S(1)} %pad_maximum_fusion.4), channel_id=1, source_target_pairs={{0,192},{1,25},{8,200},{9,17},{16,208},{17,9},{24,216},{25,1},{64,... | collective-permute-start | bytes 3145736 | tf_op jit(solution)/shard_map/ppermute | solution.py:29
  29.8 13.9 %collective-permute-start.5 = (bf16[4,64,2048]{2,1,0:T(8,128)(2,1)S(1)}, bf16[4,64,2048]{2,1,0:T(8,128)(2,1)S(1)}, u32[]{:S(2)}, u32[]{:S(2)}) collective-permute-start(bf16[4,64,2048]{2,1,0:T(8,128)(2,1)S(1)} %pad_maximum_fusion.4), channel_id=1, source_target_pairs={{0,64},{1,9},{8,72},{9,1},{16,80},{17,25},{24,88},{25,17},{64,0},{... | collective-permute-start | bytes 3145736 | tf_op jit(solution)/shard_map/ppermute | solution.py:29
  42.5 9.2 %collective-permute-start.9 = (bf16[2,64,2048]{2,1,0:T(8,128)(2,1)S(1)}, bf16[2,64,2048]{2,1,0:T(8,128)(2,1)S(1)}, u32[]{:S(2)}, u32[]{:S(2)}) collective-permute-start(bf16[2,64,2048]{2,1,0:T(8,128)(2,1)S(1)} %slice.124), channel_id=1, source_target_pairs={{0,64},{1,9},{8,72},{9,1},{16,80},{17,25},{24,88},{25,17},{64,0},{... | collective-permute-start | bytes 1572872 | tf_op jit(solution)/shard_map/ppermute | solution.py:29
  43.8 9.6 %collective-permute-start.8 = (bf16[2,64,2048]{2,1,0:T(8,128)(2,1)S(1)}, bf16[2,64,2048]{2,1,0:T(8,128)(2,1)S(1)}, u32[]{:S(2)}, u32[]{:S(2)}) collective-permute-start(bf16[2,64,2048]{2,1,0:T(8,128)(2,1)S(1)} %slice.123), channel_id=1, source_target_pairs={{0,192},{1,25},{8,200},{9,17},{16,208},{17,9},{24,216},{25,1},{64,... | collective-permute-start | bytes 1572872 | tf_op jit(solution)/shard_map/ppermute | solution.py:29
  56.6 21.9 %collective-permute-start.10 = (bf16[4,64,1024]{2,1,0:T(8,128)(2,1)}, bf16[4,64,1024]{2,1,0:T(8,128)(2,1)}, u32[]{:S(2)}, u32[]{:S(2)}) collective-permute-start(bf16[4,64,1024]{2,1,0:T(8,128)(2,1)} %get-tuple-element.21), channel_id=1, source_target_pairs={{0,2},{2,0},{4,6},{6,4},{1,3},{3,1},{5,7},{7,5},{8,10},{10,8},{12,... | collective-permute-start | bytes 1572872 | tf_op jit(solution)/shard_map/ppermute | solution.py:88
  57.8 21.1 %collective-permute-start.11 = (bf16[4,64,1024]{2,1,0:T(8,128)(2,1)S(1)}, bf16[4,64,1024]{2,1,0:T(8,128)(2,1)}, u32[]{:S(2)}, u32[]{:S(2)}) collective-permute-start(bf16[4,64,1024]{2,1,0:T(8,128)(2,1)S(1)} %get-tuple-element.22), channel_id=1, source_target_pairs={{0,4},{2,6},{4,0},{6,2},{1,5},{3,7},{5,1},{7,3},{8,12},{10,14},{12... | collective-permute-start | bytes 1572872 | tf_op jit(solution)/shard_map/ppermute | solution.py:88
  59.0 33.7 %collective-permute-start.12 = (bf16[4,64,1024]{2,1,0:T(8,128)(2,1)S(1)}, bf16[4,64,1024]{2,1,0:T(8,128)(2,1)}, u32[]{:S(2)}, u32[]{:S(2)}) collective-permute-start(bf16[4,64,1024]{2,1,0:T(8,128)(2,1)S(1)} %get-tuple-element.23), channel_id=1, source_target_pairs={{0,6},{2,4},{4,2},{6,0},{1,7},{3,5},{5,3},{7,1},{8,14},{10,12},{12... | collective-permute-start | bytes 1572872 | tf_op jit(solution)/shard_map/ppermute | solution.py:88
  94.8 28.0 %collective-permute-start.15 = (bf16[4,64,1024]{2,1,0:T(8,128)(2,1)S(1)}, bf16[4,64,1024]{2,1,0:T(8,128)(2,1)S(1)}, u32[]{:S(2)}, u32[]{:S(2)}) collective-permute-start(bf16[4,64,1024]{2,1,0:T(8,128)(2,1)S(1)} %pad_maximum_fusion.8), channel_id=1, source_target_pairs={{0,6},{2,4},{4,2},{6,0},{1,7},{3,5},{5,3},{7,1},{8,14},{10,12},{12... | collective-permute-start | bytes 1572872 | tf_op jit(solution)/shard_map/ppermute | solution.py:99
  96.5 55.7 %collective-permute-start.14 = (bf16[4,64,1024]{2,1,0:T(8,128)(2,1)S(1)}, bf16[4,64,1024]{2,1,0:T(8,128)(2,1)S(1)}, u32[]{:S(2)}, u32[]{:S(2)}) collective-permute-start(bf16[4,64,1024]{2,1,0:T(8,128)(2,1)S(1)} %pad_maximum_fusion.8), channel_id=1, source_target_pairs={{0,4},{2,6},{4,0},{6,2},{1,5},{3,7},{5,1},{7,3},{8,12},{10,14},{12... | collective-permute-start | bytes 1572872 | tf_op jit(solution)/shard_map/ppermute | solution.py:99
  119.1 33.1 %collective-permute-start.13 = (bf16[4,64,1024]{2,1,0:T(8,128)(2,1)S(1)}, bf16[4,64,1024]{2,1,0:T(8,128)(2,1)S(1)}, u32[]{:S(2)}, u32[]{:S(2)}) collective-permute-start(bf16[4,64,1024]{2,1,0:T(8,128)(2,1)S(1)} %pad_maximum_fusion.8), channel_id=1, source_target_pairs={{0,2},{2,0},{4,6},{6,4},{1,3},{3,1},{5,7},{7,5},{8,10},{10,8},{12,... | collective-permute-start | bytes 1572872 | tf_op jit(solution)/shard_map/ppermute | solution.py:99
  119.3 49.5 %collective-permute-start.20 = (bf16[1024,1024]{1,0:T(8,128)(2,1)S(1)}, bf16[1024,1024]{1,0:T(8,128)(2,1)S(1)}, u32[]{:S(2)}, u32[]{:S(2)}) collective-permute-start(bf16[1024,1024]{1,0:T(8,128)(2,1)S(1)} %pad_maximum_fusion.3), channel_id=1, source_target_pairs={{0,1},{1,0},{2,3},{3,2},{4,5},{5,4},{6,7},{7,6},{8,9},{9,8},{10,11... | collective-permute-start | bytes 6291464 | tf_op jit(solution)/shard_map/ppermute | solution.py:120
  156.6 10.2 %collective-permute-start.18 = (bf16[2,64,2048]{2,1,0:T(8,128)(2,1)S(1)}, bf16[2,64,2048]{2,1,0:T(8,128)(2,1)S(1)}, u32[]{:S(2)}, u32[]{:S(2)}) collective-permute-start(bf16[2,64,2048]{2,1,0:T(8,128)(2,1)S(1)} %get-tuple-element.55), channel_id=1, source_target_pairs={{0,64},{1,9},{8,72},{9,1},{16,80},{17,25},{24,88},{25,17},{64,0},{... | collective-permute-start | bytes 1572872 | tf_op jit(solution)/shard_map/ppermute | solution.py:29
  156.7 9.6 %collective-permute-start.16 = (bf16[2,64,2048]{2,1,0:T(8,128)(2,1)S(1)}, bf16[2,64,2048]{2,1,0:T(8,128)(2,1)S(1)}, u32[]{:S(2)}, u32[]{:S(2)}) collective-permute-start(bf16[2,64,2048]{2,1,0:T(8,128)(2,1)S(1)} %get-tuple-element.56), channel_id=1, source_target_pairs={{0,192},{1,25},{8,200},{9,17},{16,208},{17,9},{24,216},{25,1},{64,... | collective-permute-start | bytes 1572872 | tf_op jit(solution)/shard_map/ppermute | solution.py:29
  157.5 11.3 %collective-permute-start.21 = (bf16[1024,1024]{1,0:T(8,128)(2,1)S(1)}, bf16[1024,1024]{1,0:T(8,128)(2,1)}, u32[]{:S(2)}, u32[]{:S(2)}) collective-permute-start(bf16[1024,1024]{1,0:T(8,128)(2,1)S(1)} %bitcast.91), channel_id=1, source_target_pairs={{0,1},{1,0},{2,3},{3,2},{4,5},{5,4},{6,7},{7,6},{8,9},{9,8},{10,11... | collective-permute-start | bytes 6291464 | tf_op jit(solution)/shard_map/ppermute | solution.py:121
  166.6 14.0 %collective-permute-start.17 = (bf16[4,64,2048]{2,1,0:T(8,128)(2,1)S(1)}, bf16[4,64,2048]{2,1,0:T(8,128)(2,1)S(1)}, u32[]{:S(2)}, u32[]{:S(2)}) collective-permute-start(bf16[4,64,2048]{2,1,0:T(8,128)(2,1)S(1)} %pad_maximum_fusion.6), channel_id=1, source_target_pairs={{0,64},{1,9},{8,72},{9,1},{16,80},{17,25},{24,88},{25,17},{64,0},{... | collective-permute-start | bytes 3145736 | tf_op jit(solution)/shard_map/ppermute | solution.py:29
  167.1 15.5 %collective-permute-start.19 = (bf16[4,64,2048]{2,1,0:T(8,128)(2,1)S(1)}, bf16[4,64,2048]{2,1,0:T(8,128)(2,1)S(1)}, u32[]{:S(2)}, u32[]{:S(2)}) collective-permute-start(bf16[4,64,2048]{2,1,0:T(8,128)(2,1)S(1)} %pad_maximum_fusion.7), channel_id=1, source_target_pairs={{0,192},{1,25},{8,200},{9,17},{16,208},{17,9},{24,216},{25,1},{64,... | collective-permute-start | bytes 3145736 | tf_op jit(solution)/shard_map/ppermute | solution.py:29
  183.9 8.1 %collective-permute-start.24 = (bf16[64,2048]{1,0:T(8,128)(2,1)}, bf16[64,2048]{1,0:T(8,128)(2,1)S(1)}, u32[]{:S(2)}, u32[]{:S(2)}) collective-permute-start(bf16[64,2048]{1,0:T(8,128)(2,1)} %get-tuple-element.50), channel_id=1, source_target_pairs={{0,16},{1,129},{8,24},{9,137},{16,0},{17,145},{24,8},{25,153},{64,... | collective-permute-start | bytes 786440 | tf_op jit(solution)/shard_map/ppermute | solution.py:29
  184.8 8.9 %collective-permute-start.23 = (bf16[64,2048]{1,0:T(8,128)(2,1)}, bf16[64,2048]{1,0:T(8,128)(2,1)S(1)}, u32[]{:S(2)}, u32[]{:S(2)}) collective-permute-start(bf16[64,2048]{1,0:T(8,128)(2,1)} %get-tuple-element.51), channel_id=1, source_target_pairs={{0,24},{1,193},{8,16},{9,201},{16,8},{17,209},{24,0},{25,217},{64,... | collective-permute-start | bytes 786440 | tf_op jit(solution)/shard_map/ppermute | solution.py:29
  194.8 13.8 %collective-permute-start.26 = (bf16[64,1024]{1,0:T(8,128)(2,1)S(1)}, bf16[64,1024]{1,0:T(8,128)(2,1)S(1)}, u32[]{:S(2)}, u32[]{:S(2)}) collective-permute-start(bf16[64,1024]{1,0:T(8,128)(2,1)S(1)} %get-tuple-element.31), channel_id=1, source_target_pairs={{32,0},{1,33},{0,1},{33,32},{34,2},{3,35},{2,3},{35,34},{36,4},{5,... | collective-permute-start | bytes 393224 | tf_op jit(solution)/shard_map/ppermute | solution.py:140
  195.2 15.3 %collective-permute-start.25 = (bf16[64,1024]{1,0:T(8,128)(2,1)S(1)}, bf16[64,1024]{1,0:T(8,128)(2,1)S(1)}, u32[]{:S(2)}, u32[]{:S(2)}) collective-permute-start(bf16[64,1024]{1,0:T(8,128)(2,1)S(1)} %get-tuple-element.32), channel_id=1, source_target_pairs={{1,32},{32,1},{3,34},{34,3},{5,36},{36,5},{7,38},{38,7},{9,40},{40... | collective-permute-start | bytes 393224 | tf_op jit(solution)/shard_map/ppermute | solution.py:141
  (9 other events, 69.0 us)

commit v5 on v4

--- a/solution.py
+++ b/solution.py
@@ -82,9 +82,9 @@
         return jnp.where(core0, major, minor)
 
     total, *sends = lax.optimization_barrier(
-        (slab(0), *(slab(k).astype(BF16) for k in (1, 2, 3)))
+        (slab(0), *(slab(k).astype(BF16) for k in (3, 2, 1)))
     )
-    for k, send in zip((1, 2, 3), sends):
+    for k, send in zip((3, 2, 1), sends):
         total = total + lax.ppermute(send, "zl", xor_perm(4, k)).astype(F32)
     gate_pre, up_pre = total[..., :half], total[..., half:]
     sigmoid = jax.nn.sigmoid(gate_pre)

time: 212 us -> 210 us (level)
  starting transfers between devices: 74 us -> 53.2 us
  waiting for transfers between devices: 93.3 us -> 112 us
    ppermute x3, starting transfers between devices: 24.2 us -> 3.63 us  [on_device(): lax.ppermute(grads, 'zl', xor_perm(4, k))]
    ppermute x3, waiting for transfers between devices: 30.3 us -> 42.1 us  [on_device(): total = total + lax.ppermute(send, 'zl', xor_perm(4, k)).astype(F32)]
    ppermute x3, waiting for transfers between devices: 29.3 us -> 36.6 us  [on_device(): lax.ppermute(grads, 'zl', xor_perm(4, k))]
    ppermute x1, starting transfers between devices: 12.6 us -> 10.4 us  [on_device(): recv_b = lax.ppermute(g_sib, ('zh', 'c'), fwd_b)]
where the time goes in v5:
time: 210 us; the launch traced here: 209 us
  waiting for transfers between devices  112 us (53%)
  starting transfers between devices  53.2 us (25%)
  local copies, waits for them, and re-layouts  17.3 us (8%)
  matrix products  16.9 us (8%)
  other arithmetic  8.45 us (4%)
    ppermute x3, waiting for transfers between devices, on_device(): total = total + lax.ppermute(send, 'zl', xor_perm(4, k)).astype(F32)  42.1 us
    ppermute x3, waiting for transfers between devices, on_device(): lax.ppermute(grads, 'zl', xor_perm(4, k))  36.6 us
    ppermute x14, waiting for transfers between devices, send_plane(): return lax.ppermute(value, ('y', 'x', 'c'), plane_perm(k, x_core))  29.4 us
    ppermute x14, starting transfers between devices, send_plane(): return lax.ppermute(value, ('y', 'x', 'c'), plane_perm(k, x_core))  14.9 us
    ppermute x1, starting transfers between devices, on_device(): recv_b = lax.ppermute(g_sib, ('zh', 'c'), fwd_b)  10.4 us
    dot_general x1, matrix products, on_device(): lax.dot_general(jnp.concatenate([first[:, :feats], last[:, :feats], t_sib...  7.52 us
    ppermute x1, starting transfers between devices, on_device(): recv_b = lax.ppermute(tokens, ('zh', 'c'), fwd_b)  6.98 us
    unnamed x18, local copies, waits for them, and re-layouts  5.78 us
  transfers between devices with their start and end apart: 27, of which 16 were waited for; matrix products, arithmetic and copies ran while one was open for 16% of the time, Pallas kernels for 0%

profile of v5, /device:TPU:1, one launch (start us, length us, event | category | flops | bytes accessed | tf_op | source)
XLA Modules:
  0.0 209.0 jit_solution(750320153992173709)
XLA Ops:
  0.6 3.3 %collective-permute-start = (bf16[64,1024]{1,0:T(8,128)(2,1)}, bf16[64,1024]{1,0:T(8,128)(2,1)S(1)}, u32[]{:S(2)}, u32[]{:S(2)}) collective-permute-start(bf16[64,1024]{1,0:T(8,128)(2,1)} %param.3), channel_id=1, source_target_pairs={{0,32},{33,1},{1,0},{32,33},{2,34},{35,3},{3,2},{34,35},{4,36},{37... | collective-permute-start | bytes 393224 | tf_op jit(solution)/shard_map/ppermute | solution.py:50
  4.0 7.0 %collective-permute-start.1 = (bf16[64,1024]{1,0:T(8,128)(2,1)}, bf16[64,1024]{1,0:T(8,128)(2,1)S(1)}, u32[]{:S(2)}, u32[]{:S(2)}) collective-permute-start(bf16[64,1024]{1,0:T(8,128)(2,1)} %param.3), channel_id=1, source_target_pairs={{1,32},{32,1},{3,34},{34,3},{5,36},{36,5},{7,38},{38,7},{9,40},{40... | collective-permute-start | bytes 393224 | tf_op jit(solution)/shard_map/ppermute | solution.py:51
  11.0 2.1 %copy.10 = bf16[128,8,2,512]{3,1,2,0:T(8,128)(2,1)S(1)} copy(bf16[128,8,2,512]{3,2,1,0:T(2,128)(2,1)} %bitcast.101) | data formatting | bytes 4194304
  16.1 2.7 %collective-permute-start.3 = (bf16[64,2048]{1,0:T(8,128)(2,1)}, bf16[64,2048]{1,0:T(8,128)(2,1)S(1)}, u32[]{:S(2)}, u32[]{:S(2)}) collective-permute-start(bf16[64,2048]{1,0:T(8,128)(2,1)} %get-tuple-element.67), channel_id=1, source_target_pairs={{0,24},{1,193},{8,16},{9,201},{16,8},{17,209},{24,0},{25,217},{64,... | collective-permute-start | bytes 786440 | tf_op jit(solution)/shard_map/ppermute | solution.py:29
  24.6 2.5 %collective-permute-done.4 = bf16[64,2048]{1,0:T(8,128)(2,1)S(1)} collective-permute-done((bf16[64,2048]{1,0:T(8,128)(2,1)}, bf16[64,2048]{1,0:T(8,128)(2,1)S(1)}, u32[]{:S(2)}, u32[]{:S(2)}) %collective-permute-start.4) | collective-permute-done | bytes 262176 | tf_op jit(solution)/shard_map/ppermute | solution.py:29
  27.2 2.6 %collective-permute-start.6 = (bf16[4,64,2048]{2,1,0:T(8,128)(2,1)S(1)}, bf16[4,64,2048]{2,1,0:T(8,128)(2,1)S(1)}, u32[]{:S(2)}, u32[]{:S(2)}) collective-permute-start(bf16[4,64,2048]{2,1,0:T(8,128)(2,1)S(1)} %pad_maximum_fusion.4), channel_id=1, source_target_pairs={{0,192},{1,25},{8,200},{9,17},{16,208},{17,9},{24,216},{25,1},{64,... | collective-permute-start | bytes 3145736 | tf_op jit(solution)/shard_map/ppermute | solution.py:29
  29.9 12.6 %collective-permute-done.6 = bf16[4,64,2048]{2,1,0:T(8,128)(2,1)S(1)} collective-permute-done((bf16[4,64,2048]{2,1,0:T(8,128)(2,1)S(1)}, bf16[4,64,2048]{2,1,0:T(8,128)(2,1)S(1)}, u32[]{:S(2)}, u32[]{:S(2)}) %collective-permute-start.6) | collective-permute-done | bytes 1048608 | tf_op jit(solution)/shard_map/ppermute | solution.py:29
  45.4 2.9 %constant_dynamic-update-slice_fusion.6 = bf16[2048,1024]{1,0:T(8,128)(2,1)S(1)} fusion(bf16[2048,1024]{1,0:T(8,128)(2,1)S(1)} %copy-done.1, bf16[1024,1024]{1,0:T(8,128)(2,1)} %collective-permute-done.7), kind=kLoop, calls=%fused_computation.67 | loop fusion | bytes 4194304 | tf_op jit(solution)/shard_map/concatenate | solution.py:58
  48.3 3.4 %fusion.40 = f32[768,1024]{1,0:T(8,128)S(1)} fusion(bf16[768,2048]{1,0:T(8,128)(2,1)S(1)} %bitcast.97, bf16[2048,1024]{1,0:T(8,128)(2,1)S(1)} %constant_dynamic-update-slice_fusion.6), kind=kOutput, calls=%fused_computation.90 | convolution fusion | flops 3221225472 | bytes 10485760 | tf_op jit(solution)/shard_map/dot_general | solution.py:71
  60.2 2.2 %fusion.35 = (bf16[768,1024]{1,0:T(8,128)(2,1)S(1)}, bf16[768,1024]{1,0:T(8,128)(2,1)S(1)}) fusion(bf16[768,2048]{1,0:T(8,128)(2,1)} %bitcast.98), kind=kLoop, calls=%fused_computation.85 | loop fusion | bytes 6291456 | tf_op jit(solution)/shard_map/slice | solution.py:123
  62.4 6.8 %collective-permute-done.10 = bf16[4,64,1024]{2,1,0:T(8,128)(2,1)} collective-permute-done((bf16[4,64,1024]{2,1,0:T(8,128)(2,1)}, bf16[4,64,1024]{2,1,0:T(8,128)(2,1)}, u32[]{:S(2)}, u32[]{:S(2)}) %collective-permute-start.10) | collective-permute-done | bytes 524320 | tf_op jit(solution)/shard_map/ppermute | solution.py:88
  69.2 35.3 %collective-permute-done.11 = bf16[4,64,1024]{2,1,0:T(8,128)(2,1)} collective-permute-done((bf16[4,64,1024]{2,1,0:T(8,128)(2,1)S(1)}, bf16[4,64,1024]{2,1,0:T(8,128)(2,1)}, u32[]{:S(2)}, u32[]{:S(2)}) %collective-permute-start.11) | collective-permute-done | bytes 524320 | tf_op jit(solution)/shard_map/ppermute | solution.py:88
  107.5 2.7 %collective-permute-start.13 = (bf16[4,64,1024]{2,1,0:T(8,128)(2,1)S(1)}, bf16[4,64,1024]{2,1,0:T(8,128)(2,1)S(1)}, u32[]{:S(2)}, u32[]{:S(2)}) collective-permute-start(bf16[4,64,1024]{2,1,0:T(8,128)(2,1)S(1)} %pad_maximum_fusion.8), channel_id=1, source_target_pairs={{0,2},{2,0},{4,6},{6,4},{1,3},{3,1},{5,7},{7,5},{8,10},{10,8},{12,... | collective-permute-start | bytes 1572872 | tf_op jit(solution)/shard_map/ppermute | solution.py:99
  110.5 2.4 %collective-permute-start.20 = (bf16[1024,1024]{1,0:T(8,128)(2,1)S(1)}, bf16[1024,1024]{1,0:T(8,128)(2,1)S(1)}, u32[]{:S(2)}, u32[]{:S(2)}) collective-permute-start(bf16[1024,1024]{1,0:T(8,128)(2,1)S(1)} %pad_maximum_fusion.3), channel_id=1, source_target_pairs={{0,1},{1,0},{2,3},{3,2},{4,5},{5,4},{6,7},{7,6},{8,9},{9,8},{10,11... | collective-permute-start | bytes 6291464 | tf_op jit(solution)/shard_map/ppermute | solution.py:120
  112.9 7.7 %collective-permute-done.15 = bf16[4,64,1024]{2,1,0:T(8,128)(2,1)S(1)} collective-permute-done((bf16[4,64,1024]{2,1,0:T(8,128)(2,1)S(1)}, bf16[4,64,1024]{2,1,0:T(8,128)(2,1)S(1)}, u32[]{:S(2)}, u32[]{:S(2)}) %collective-permute-start.15) | collective-permute-done | bytes 524320 | tf_op jit(solution)/shard_map/ppermute | solution.py:99
  120.6 28.9 %collective-permute-done.14 = bf16[4,64,1024]{2,1,0:T(8,128)(2,1)S(1)} collective-permute-done((bf16[4,64,1024]{2,1,0:T(8,128)(2,1)S(1)}, bf16[4,64,1024]{2,1,0:T(8,128)(2,1)S(1)}, u32[]{:S(2)}, u32[]{:S(2)}) %collective-permute-start.14) | collective-permute-done | bytes 524320 | tf_op jit(solution)/shard_map/ppermute | solution.py:99
  154.8 5.5 %collective-permute-start.21 = (bf16[1024,1024]{1,0:T(8,128)(2,1)S(1)}, bf16[1024,1024]{1,0:T(8,128)(2,1)}, u32[]{:S(2)}, u32[]{:S(2)}) collective-permute-start(bf16[1024,1024]{1,0:T(8,128)(2,1)S(1)} %bitcast.91), channel_id=1, source_target_pairs={{0,1},{1,0},{2,3},{3,2},{4,5},{5,4},{6,7},{7,6},{8,9},{9,8},{10,11... | collective-permute-start | bytes 6291464 | tf_op jit(solution)/shard_map/ppermute | solution.py:121
  160.3 3.4 %fusion.39 = (bf16[768,2048]{1,0:T(8,128)(2,1)S(1)}, f32[768,2048]{1,0:T(8,128)S(1)}) fusion(bf16[768,1024]{1,0:T(8,128)(2,1)S(1)} %bitcast.104, bf16[2048,1024]{1,0:T(8,128)(2,1)S(1)} %copy-done.3), kind=kOutput, calls=%fused_computation.89 | convolution fusion | flops 3222798336 | bytes 15204352 | tf_op jit(solution)/shard_map/dot_general | solution.py:106
  166.9 7.5 %fusion.14 = bf16[1024,1024]{1,0:T(8,128)(2,1)} fusion(bf16[1024,1024]{1,0:T(8,128)(2,1)} %collective-permute-done.21, bf16[1024,1024]{1,0:T(8,128)(2,1)S(1)} %bitcast.92, bf16[1024,1024]{1,0:T(8,128)(2,1)S(1)} %collective-permute-done.20, bf16[256,1024]{1,0:T(8,128)(2,1)S(1)} %get-tuple-element.53, bf16[768,1024]{1,0:T(8,128)(2,1)S(1)} %get-tuple-element.40), kind=kOutput, calls=%fused_computation.18 | convolution fusion | flops 4316987392 | bytes 10485760 | tf_op jit(solution)/shard_map/dot_general | solution.py:122
  174.4 4.1 %collective-permute-done.17 = bf16[4,64,2048]{2,1,0:T(8,128)(2,1)S(1)} collective-permute-done((bf16[4,64,2048]{2,1,0:T(8,128)(2,1)S(1)}, bf16[4,64,2048]{2,1,0:T(8,128)(2,1)S(1)}, u32[]{:S(2)}, u32[]{:S(2)}) %collective-permute-start.17) | collective-permute-done | bytes 1048608 | tf_op jit(solution)/shard_map/ppermute | solution.py:29
  182.5 2.5 %collective-permute-start.23 = (bf16[64,2048]{1,0:T(8,128)(2,1)}, bf16[64,2048]{1,0:T(8,128)(2,1)S(1)}, u32[]{:S(2)}, u32[]{:S(2)}) collective-permute-start(bf16[64,2048]{1,0:T(8,128)(2,1)} %get-tuple-element.51), channel_id=1, source_target_pairs={{0,24},{1,193},{8,16},{9,201},{16,8},{17,209},{24,0},{25,217},{64,... | collective-permute-start | bytes 786440 | tf_op jit(solution)/shard_map/ppermute | solution.py:29
  185.6 4.5 %reshape.88 = bf16[1024,2,512]{2,1,0:T(2,128)(2,1)} reshape(bf16[1024,1024]{1,0:T(8,128)(2,1)} %fusion.14) | data formatting | bytes 4194304 | tf_op jit(solution)/shard_map/reshape | solution.py:133
  192.8 2.4 %collective-permute-start.26 = (bf16[64,1024]{1,0:T(8,128)(2,1)S(1)}, bf16[64,1024]{1,0:T(8,128)(2,1)S(1)}, u32[]{:S(2)}, u32[]{:S(2)}) collective-permute-start(bf16[64,1024]{1,0:T(8,128)(2,1)S(1)} %get-tuple-element.31), channel_id=1, source_target_pairs={{32,0},{1,33},{0,1},{33,32},{34,2},{3,35},{2,3},{35,34},{36,4},{5,... | collective-permute-start | bytes 393224 | tf_op jit(solution)/shard_map/ppermute | solution.py:140
  195.2 10.4 %collective-permute-start.25 = (bf16[64,1024]{1,0:T(8,128)(2,1)S(1)}, bf16[64,1024]{1,0:T(8,128)(2,1)S(1)}, u32[]{:S(2)}, u32[]{:S(2)}) collective-permute-start(bf16[64,1024]{1,0:T(8,128)(2,1)S(1)} %get-tuple-element.32), channel_id=1, source_target_pairs={{1,32},{32,1},{3,34},{34,3},{5,36},{36,5},{7,38},{38,7},{9,40},{40... | collective-permute-start | bytes 393224 | tf_op jit(solution)/shard_map/ppermute | solution.py:141
  (94 shorter events, 42.5 us)
Async XLA Ops:
  0.6 12.6 %collective-permute-start = (bf16[64,1024]{1,0:T(8,128)(2,1)}, bf16[64,1024]{1,0:T(8,128)(2,1)S(1)}, u32[]{:S(2)}, u32[]{:S(2)}) collective-permute-start(bf16[64,1024]{1,0:T(8,128)(2,1)} %param.3), channel_id=1, source_target_pairs={{0,32},{33,1},{1,0},{32,33},{2,34},{35,3},{3,2},{34,35},{4,36},{37... | collective-permute-start | bytes 393224 | tf_op jit(solution)/shard_map/ppermute | solution.py:50
  4.0 11.3 %collective-permute-start.1 = (bf16[64,1024]{1,0:T(8,128)(2,1)}, bf16[64,1024]{1,0:T(8,128)(2,1)S(1)}, u32[]{:S(2)}, u32[]{:S(2)}) collective-permute-start(bf16[64,1024]{1,0:T(8,128)(2,1)} %param.3), channel_id=1, source_target_pairs={{1,32},{32,1},{3,34},{34,3},{5,36},{36,5},{7,38},{38,7},{9,40},{40... | collective-permute-start | bytes 393224 | tf_op jit(solution)/shard_map/ppermute | solution.py:51
  13.1 32.3 %collective-permute-start.7 = (bf16[1024,1024]{1,0:T(8,128)(2,1)S(1)}, bf16[1024,1024]{1,0:T(8,128)(2,1)}, u32[]{:S(2)}, u32[]{:S(2)}) collective-permute-start(bf16[1024,1024]{1,0:T(8,128)(2,1)S(1)} %bitcast.89), channel_id=1, source_target_pairs={{0,1},{1,0},{2,3},{3,2},{4,5},{5,4},{6,7},{7,6},{8,9},{9,8},{10,11... | collective-permute-start | bytes 6291464 | tf_op jit(solution)/shard_map/ppermute | solution.py:57
  18.8 8.3 %collective-permute-start.4 = (bf16[64,2048]{1,0:T(8,128)(2,1)}, bf16[64,2048]{1,0:T(8,128)(2,1)S(1)}, u32[]{:S(2)}, u32[]{:S(2)}) collective-permute-start(bf16[64,2048]{1,0:T(8,128)(2,1)} %get-tuple-element.67), channel_id=1, source_target_pairs={{0,16},{1,129},{8,24},{9,137},{16,0},{17,145},{24,8},{25,153},{64,... | collective-permute-start | bytes 786440 | tf_op jit(solution)/shard_map/ppermute | solution.py:29
  27.2 15.2 %collective-permute-start.6 = (bf16[4,64,2048]{2,1,0:T(8,128)(2,1)S(1)}, bf16[4,64,2048]{2,1,0:T(8,128)(2,1)S(1)}, u32[]{:S(2)}, u32[]{:S(2)}) collective-permute-start(bf16[4,64,2048]{2,1,0:T(8,128)(2,1)S(1)} %pad_maximum_fusion.4), channel_id=1, source_target_pairs={{0,192},{1,25},{8,200},{9,17},{16,208},{17,9},{24,216},{25,1},{64,... | collective-permute-start | bytes 3145736 | tf_op jit(solution)/shard_map/ppermute | solution.py:29
  29.8 13.9 %collective-permute-start.5 = (bf16[4,64,2048]{2,1,0:T(8,128)(2,1)S(1)}, bf16[4,64,2048]{2,1,0:T(8,128)(2,1)S(1)}, u32[]{:S(2)}, u32[]{:S(2)}) collective-permute-start(bf16[4,64,2048]{2,1,0:T(8,128)(2,1)S(1)} %pad_maximum_fusion.4), channel_id=1, source_target_pairs={{0,64},{1,9},{8,72},{9,1},{16,80},{17,25},{24,88},{25,17},{64,0},{... | collective-permute-start | bytes 3145736 | tf_op jit(solution)/shard_map/ppermute | solution.py:29
  42.5 9.2 %collective-permute-start.9 = (bf16[2,64,2048]{2,1,0:T(8,128)(2,1)S(1)}, bf16[2,64,2048]{2,1,0:T(8,128)(2,1)S(1)}, u32[]{:S(2)}, u32[]{:S(2)}) collective-permute-start(bf16[2,64,2048]{2,1,0:T(8,128)(2,1)S(1)} %slice.124), channel_id=1, source_target_pairs={{0,64},{1,9},{8,72},{9,1},{16,80},{17,25},{24,88},{25,17},{64,0},{... | collective-permute-start | bytes 1572872 | tf_op jit(solution)/shard_map/ppermute | solution.py:29
  43.8 9.6 %collective-permute-start.8 = (bf16[2,64,2048]{2,1,0:T(8,128)(2,1)S(1)}, bf16[2,64,2048]{2,1,0:T(8,128)(2,1)S(1)}, u32[]{:S(2)}, u32[]{:S(2)}) collective-permute-start(bf16[2,64,2048]{2,1,0:T(8,128)(2,1)S(1)} %slice.123), channel_id=1, source_target_pairs={{0,192},{1,25},{8,200},{9,17},{16,208},{17,9},{24,216},{25,1},{64,... | collective-permute-start | bytes 1572872 | tf_op jit(solution)/shard_map/ppermute | solution.py:29
  56.6 12.6 %collective-permute-start.10 = (bf16[4,64,1024]{2,1,0:T(8,128)(2,1)}, bf16[4,64,1024]{2,1,0:T(8,128)(2,1)}, u32[]{:S(2)}, u32[]{:S(2)}) collective-permute-start(bf16[4,64,1024]{2,1,0:T(8,128)(2,1)} %get-tuple-element.21), channel_id=1, source_target_pairs={{0,6},{2,4},{4,2},{6,0},{1,7},{3,5},{5,3},{7,1},{8,14},{10,12},{12... | collective-permute-start | bytes 1572872 | tf_op jit(solution)/shard_map/ppermute | solution.py:88
  58.8 45.7 %collective-permute-start.11 = (bf16[4,64,1024]{2,1,0:T(8,128)(2,1)S(1)}, bf16[4,64,1024]{2,1,0:T(8,128)(2,1)}, u32[]{:S(2)}, u32[]{:S(2)}) collective-permute-start(bf16[4,64,1024]{2,1,0:T(8,128)(2,1)S(1)} %get-tuple-element.22), channel_id=1, source_target_pairs={{0,4},{2,6},{4,0},{6,2},{1,5},{3,7},{5,1},{7,3},{8,12},{10,14},{12... | collective-permute-start | bytes 1572872 | tf_op jit(solution)/shard_map/ppermute | solution.py:88
  59.0 45.5 %collective-permute-start.12 = (bf16[4,64,1024]{2,1,0:T(8,128)(2,1)S(1)}, bf16[4,64,1024]{2,1,0:T(8,128)(2,1)}, u32[]{:S(2)}, u32[]{:S(2)}) collective-permute-start(bf16[4,64,1024]{2,1,0:T(8,128)(2,1)S(1)} %get-tuple-element.23), channel_id=1, source_target_pairs={{0,2},{2,0},{4,6},{6,4},{1,3},{3,1},{5,7},{7,5},{8,10},{10,8},{12,... | collective-permute-start | bytes 1572872 | tf_op jit(solution)/shard_map/ppermute | solution.py:88
  106.6 14.0 %collective-permute-start.15 = (bf16[4,64,1024]{2,1,0:T(8,128)(2,1)S(1)}, bf16[4,64,1024]{2,1,0:T(8,128)(2,1)S(1)}, u32[]{:S(2)}, u32[]{:S(2)}) collective-permute-start(bf16[4,64,1024]{2,1,0:T(8,128)(2,1)S(1)} %pad_maximum_fusion.8), channel_id=1, source_target_pairs={{0,6},{2,4},{4,2},{6,0},{1,7},{3,5},{5,3},{7,1},{8,14},{10,12},{12... | collective-permute-start | bytes 1572872 | tf_op jit(solution)/shard_map/ppermute | solution.py:99
  107.5 42.0 %collective-permute-start.14 = (bf16[4,64,1024]{2,1,0:T(8,128)(2,1)S(1)}, bf16[4,64,1024]{2,1,0:T(8,128)(2,1)S(1)}, u32[]{:S(2)}, u32[]{:S(2)}) collective-permute-start(bf16[4,64,1024]{2,1,0:T(8,128)(2,1)S(1)} %pad_maximum_fusion.8), channel_id=1, source_target_pairs={{0,4},{2,6},{4,0},{6,2},{1,5},{3,7},{5,1},{7,3},{8,12},{10,14},{12... | collective-permute-start | bytes 1572872 | tf_op jit(solution)/shard_map/ppermute | solution.py:99
  107.5 42.0 %collective-permute-start.13 = (bf16[4,64,1024]{2,1,0:T(8,128)(2,1)S(1)}, bf16[4,64,1024]{2,1,0:T(8,128)(2,1)S(1)}, u32[]{:S(2)}, u32[]{:S(2)}) collective-permute-start(bf16[4,64,1024]{2,1,0:T(8,128)(2,1)S(1)} %pad_maximum_fusion.8), channel_id=1, source_target_pairs={{0,2},{2,0},{4,6},{6,4},{1,3},{3,1},{5,7},{7,5},{8,10},{10,8},{12,... | collective-permute-start | bytes 1572872 | tf_op jit(solution)/shard_map/ppermute | solution.py:99
  110.5 56.4 %collective-permute-start.20 = (bf16[1024,1024]{1,0:T(8,128)(2,1)S(1)}, bf16[1024,1024]{1,0:T(8,128)(2,1)S(1)}, u32[]{:S(2)}, u32[]{:S(2)}) collective-permute-start(bf16[1024,1024]{1,0:T(8,128)(2,1)S(1)} %pad_maximum_fusion.3), channel_id=1, source_target_pairs={{0,1},{1,0},{2,3},{3,2},{4,5},{5,4},{6,7},{7,6},{8,9},{9,8},{10,11... | collective-permute-start | bytes 6291464 | tf_op jit(solution)/shard_map/ppermute | solution.py:120
  154.0 10.6 %collective-permute-start.18 = (bf16[2,64,2048]{2,1,0:T(8,128)(2,1)S(1)}, bf16[2,64,2048]{2,1,0:T(8,128)(2,1)S(1)}, u32[]{:S(2)}, u32[]{:S(2)}) collective-permute-start(bf16[2,64,2048]{2,1,0:T(8,128)(2,1)S(1)} %get-tuple-element.55), channel_id=1, source_target_pairs={{0,64},{1,9},{8,72},{9,1},{16,80},{17,25},{24,88},{25,17},{64,0},{... | collective-permute-start | bytes 1572872 | tf_op jit(solution)/shard_map/ppermute | solution.py:29
  154.1 10.1 %collective-permute-start.16 = (bf16[2,64,2048]{2,1,0:T(8,128)(2,1)S(1)}, bf16[2,64,2048]{2,1,0:T(8,128)(2,1)S(1)}, u32[]{:S(2)}, u32[]{:S(2)}) collective-permute-start(bf16[2,64,2048]{2,1,0:T(8,128)(2,1)S(1)} %get-tuple-element.56), channel_id=1, source_target_pairs={{0,192},{1,25},{8,200},{9,17},{16,208},{17,9},{24,216},{25,1},{64,... | collective-permute-start | bytes 1572872 | tf_op jit(solution)/shard_map/ppermute | solution.py:29
  154.8 12.1 %collective-permute-start.21 = (bf16[1024,1024]{1,0:T(8,128)(2,1)S(1)}, bf16[1024,1024]{1,0:T(8,128)(2,1)}, u32[]{:S(2)}, u32[]{:S(2)}) collective-permute-start(bf16[1024,1024]{1,0:T(8,128)(2,1)S(1)} %bitcast.91), channel_id=1, source_target_pairs={{0,1},{1,0},{2,3},{3,2},{4,5},{5,4},{6,7},{7,6},{8,9},{9,8},{10,11... | collective-permute-start | bytes 6291464 | tf_op jit(solution)/shard_map/ppermute | solution.py:121
  164.4 14.0 %collective-permute-start.17 = (bf16[4,64,2048]{2,1,0:T(8,128)(2,1)S(1)}, bf16[4,64,2048]{2,1,0:T(8,128)(2,1)S(1)}, u32[]{:S(2)}, u32[]{:S(2)}) collective-permute-start(bf16[4,64,2048]{2,1,0:T(8,128)(2,1)S(1)} %pad_maximum_fusion.6), channel_id=1, source_target_pairs={{0,64},{1,9},{8,72},{9,1},{16,80},{17,25},{24,88},{25,17},{64,0},{... | collective-permute-start | bytes 3145736 | tf_op jit(solution)/shard_map/ppermute | solution.py:29
  164.8 15.5 %collective-permute-start.19 = (bf16[4,64,2048]{2,1,0:T(8,128)(2,1)S(1)}, bf16[4,64,2048]{2,1,0:T(8,128)(2,1)S(1)}, u32[]{:S(2)}, u32[]{:S(2)}) collective-permute-start(bf16[4,64,2048]{2,1,0:T(8,128)(2,1)S(1)} %pad_maximum_fusion.7), channel_id=1, source_target_pairs={{0,192},{1,25},{8,200},{9,17},{16,208},{17,9},{24,216},{25,1},{64,... | collective-permute-start | bytes 3145736 | tf_op jit(solution)/shard_map/ppermute | solution.py:29
  181.7 8.4 %collective-permute-start.24 = (bf16[64,2048]{1,0:T(8,128)(2,1)}, bf16[64,2048]{1,0:T(8,128)(2,1)S(1)}, u32[]{:S(2)}, u32[]{:S(2)}) collective-permute-start(bf16[64,2048]{1,0:T(8,128)(2,1)} %get-tuple-element.50), channel_id=1, source_target_pairs={{0,16},{1,129},{8,24},{9,137},{16,0},{17,145},{24,8},{25,153},{64,... | collective-permute-start | bytes 786440 | tf_op jit(solution)/shard_map/ppermute | solution.py:29
  182.5 9.0 %collective-permute-start.23 = (bf16[64,2048]{1,0:T(8,128)(2,1)}, bf16[64,2048]{1,0:T(8,128)(2,1)S(1)}, u32[]{:S(2)}, u32[]{:S(2)}) collective-permute-start(bf16[64,2048]{1,0:T(8,128)(2,1)} %get-tuple-element.51), channel_id=1, source_target_pairs={{0,24},{1,193},{8,16},{9,201},{16,8},{17,209},{24,0},{25,217},{64,... | collective-permute-start | bytes 786440 | tf_op jit(solution)/shard_map/ppermute | solution.py:29
  192.8 13.6 %collective-permute-start.26 = (bf16[64,1024]{1,0:T(8,128)(2,1)S(1)}, bf16[64,1024]{1,0:T(8,128)(2,1)S(1)}, u32[]{:S(2)}, u32[]{:S(2)}) collective-permute-start(bf16[64,1024]{1,0:T(8,128)(2,1)S(1)} %get-tuple-element.31), channel_id=1, source_target_pairs={{32,0},{1,33},{0,1},{33,32},{34,2},{3,35},{2,3},{35,34},{36,4},{5,... | collective-permute-start | bytes 393224 | tf_op jit(solution)/shard_map/ppermute | solution.py:140
  195.2 13.0 %collective-permute-start.25 = (bf16[64,1024]{1,0:T(8,128)(2,1)S(1)}, bf16[64,1024]{1,0:T(8,128)(2,1)S(1)}, u32[]{:S(2)}, u32[]{:S(2)}) collective-permute-start(bf16[64,1024]{1,0:T(8,128)(2,1)S(1)} %get-tuple-element.32), channel_id=1, source_target_pairs={{1,32},{32,1},{3,34},{34,3},{5,36},{36,5},{7,38},{38,7},{9,40},{40... | collective-permute-start | bytes 393224 | tf_op jit(solution)/shard_map/ppermute | solution.py:141
  (9 other events, 69.0 us)
